TPU v7x, 32 devices: a whole 2x2x4 slice. The times are simulated.
32 devices in a mesh: wide: 16 (over z, y, x), narrow: 2 (over core).
Axes of the slice: x: 2, y: 2, z: 4, core: 2. Of those that a mesh axis runs over, the one named last changes fastest.
Arguments:
- tokens: bfloat16 [32, 8192], P('wide', 'narrow'), may hold values from -6 to 6
- cotangent: bfloat16 [32, 8192], P('wide', 'narrow'), may hold values from -6 to 6
- gate_tiles: bfloat16 [2, 16, 48, 128, 128], P('narrow', 'wide'), may hold values from -0.109375 to 0.109375
- up_tiles: bfloat16 [2, 16, 48, 128, 128], P('narrow', 'wide'), may hold values from -0.109375 to 0.109375
- down_tiles: bfloat16 [2, 16, 48, 128, 128], P('narrow', 'wide'), may hold values from -0.125 to 0.125
- kept_slots: int32 [3, 2, 16, 48], P(None, 'narrow', 'wide'), may hold values from 0 to 95, as said below
- kept_counts: int32 [3, 2, 16], P(None, 'narrow', 'wide'), may hold values from 12 to 48, as said below
Outputs:
- layer_out: bfloat16 [32, 8192], P('wide', 'narrow')
- input_grad: bfloat16 [32, 8192], P('wide', 'narrow')
- gate_grad: bfloat16 [2, 16, 48, 128, 128], P('narrow', 'wide')
- up_grad: bfloat16 [2, 16, 48, 128, 128], P('narrow', 'wide')
- down_grad: bfloat16 [2, 16, 48, 128, 128], P('narrow', 'wide')
Inputs may be any that keep to these rules, and one draw needn't show every extreme that they name: `kept_slots`: for each matrix and device the first 48 entries are distinct local tile positions. `kept_counts`: for each matrix some device keeps exactly 48 tiles.
All inputs are finite; a program needn't handle non-finite values.
Results may differ from a plain program's by a relative error of at most 0.005.
Values may be sent and summed in bfloat16 or wider, within the bound.
No kernel may reach another device: no remote copies, remote signals or barrier semaphores. Data moves between devices by JAX's collectives and lax.ppermute only.
A program may use at most 64 MiB of HBM per device.

v0:
```python
import functools

import jax
import jax.numpy as jnp
from jax import lax
from jax.experimental import pallas as pl
from jax.experimental.pallas import tpu as pltpu
from jax.sharding import PartitionSpec as P


HT = 3
VM = pl.BlockSpec(memory_space=pltpu.VMEM)
SM = pl.BlockSpec(memory_space=pltpu.SMEM)
HBM = pl.BlockSpec(memory_space=pltpu.HBM)
VLIM = pltpu.CompilerParams(vmem_limit_bytes=16 << 20)
F32 = jnp.float32
BF16 = jnp.bfloat16


def group_of(cap):
    for size in (8, 6, 4, 3, 2):
        if cap % size == 0:
            return size
    return 1


def lanes(index, tile):
    return pl.ds(pl.multiple_of(index * tile, tile), tile)


def live_groups(count, group):
    return lax.div(count + (group - 1), group)


def forward_kernel(group, idx, counts, panel, gate, up, down, parts):
    tile = gate.shape[-1]
    rows = panel.shape[1]

    def stacked(which, m, base):
        blocks = []
        for j in range(group):
            k = base + j
            block = idx[m, 0, k]
            col = idx[m, 1, k]
            pick = panel[which, :, lanes(block, tile)]
            zero = jnp.zeros_like(pick)
            blocks.append(
                jnp.concatenate([jnp.where(col == c, pick, zero) for c in range(HT)], axis=0)
            )
        return jnp.concatenate(blocks, axis=1)

    for m, which, ref in ((0, 0, gate), (1, 0, up), (2, 1, down)):

        def step(g, acc, m=m, which=which, ref=ref):
            base = g * group
            lhs = stacked(which, m, base)
            if m < 2:
                rhs = ref[pl.ds(base, group)].reshape(group * tile, tile)
                return acc + lax.dot_general(
                    lhs, rhs, (((1,), (0,)), ((), ())), preferred_element_type=F32
                )
            rhs = jnp.concatenate([ref[base + j] for j in range(group)], axis=1)
            return acc + lax.dot_general(
                lhs, rhs, (((1,), (1,)), ((), ())), preferred_element_type=F32
            )

        total = lax.fori_loop(
            0, live_groups(counts[m], group), step, jnp.zeros((HT * rows, tile), F32)
        )
        parts[m] = total.reshape(HT, rows, tile)


def backward_kernel(
    group, quarters, idx, counts, parts, other, gate, up, down, acts, keep, *rest
):
    sends, (out_sum, in_sum) = rest[:quarters - 1], rest[quarters - 1:]
    tile = gate.shape[-1]
    rows = parts.shape[2]
    gate_sum = parts[0] + other[0]
    up_sum = parts[1] + other[1]
    hidden_grad = parts[2] + other[2]
    sig = jax.nn.sigmoid(gate_sum)
    acts[0, :HT] = (
        hidden_grad * up_sum * sig * (1.0 + gate_sum * (1.0 - sig))
    ).astype(BF16)
    acts[1, :HT] = (hidden_grad * gate_sum * sig).astype(BF16)
    acts[2, :HT] = (gate_sum * sig * up_sum).astype(BF16)
    for m in range(3):
        acts[m, HT] = jnp.zeros((rows, tile), BF16)
    out_sum[...] = jnp.zeros_like(out_sum)
    in_sum[...] = jnp.zeros_like(in_sum)
    for m, ref, target in ((2, down, out_sum), (0, gate, in_sum), (1, up, in_sum)):

        def step(g, carry, m=m, ref=ref, target=target):
            base = g * group
            products = []
            for j in range(group):
                lhs = acts[m, idx[m, 1, base + j]]
                dims = (((1,), (0 if m == 2 else 1,)), ((), ()))
                products.append(
                    lax.dot_general(lhs, ref[base + j], dims, preferred_element_type=F32)
                )
            for j in range(group):
                where = lanes(idx[m, 0, base + j], tile)
                target[:, where] += products[j]
            return carry

        lax.fori_loop(0, live_groups(counts[m], group), step, 0)
    size = rows // quarters
    for which, total in ((0, out_sum), (1, in_sum)):
        keep[which] = total[:size]
        for q in range(1, quarters):
            sends[q - 1][which] = total[q * size:(q + 1) * size].astype(BF16)


def grad_kernel(group, m, which, idx, counts, panel, acts, out, buf, sem):
    tile = out.shape[-1]
    cap = out.shape[0]
    copies = []
    for g in range(cap // group):
        for j in range(group):
            k = g * group + j
            block = panel[which, :, lanes(idx[m, 0, k], tile)]
            act = acts[m, idx[m, 1, k]]
            left, right = (act, block) if m == 2 else (block, act)
            buf[k] = lax.dot_general(
                left, right, (((0,), (0,)), ((), ())), preferred_element_type=F32
            ).astype(BF16)
        copy = pltpu.make_async_copy(
            buf.at[pl.ds(g * group, group)], out.at[pl.ds(g * group, group)], sem.at[g]
        )
        copy.start()
        copies.append(copy)
    for copy in copies:
        copy.wait()


def load_kernel(gate_in, up_in, down_in, gate, up, down, sem):
    pairs = ((gate_in, gate), (up_in, up), (down_in, down))
    copies = [pltpu.make_async_copy(a, b, sem.at[i]) for i, (a, b) in enumerate(pairs)]
    for copy in copies:
        copy.start()
    for copy in copies:
        copy.wait()


def bits_of(size):
    assert size & (size - 1) == 0
    return [1 << i for i in range(size.bit_length() - 1)]


def stages_of(size):
    bits = bits_of(size)
    parts = [bits[i:i + 2] for i in range(0, len(bits), 2)]
    return [
        [sum(b for i, b in enumerate(part) if q >> i & 1) for q in range(1 << len(part))]
        for part in parts
    ]


def per_device(tokens, cotangent, gate_tiles, up_tiles, down_tiles, kept_slots, kept_counts):
    tile = gate_tiles.shape[-1]
    cap = gate_tiles.shape[2]
    group = group_of(cap)
    feats = tokens.shape[1]
    row_blocks = feats // tile
    n_wide = lax.axis_size("wide")
    n_narrow = lax.axis_size("narrow")
    rows = tokens.shape[0] * n_wide
    stages = stages_of(n_wide)
    quarters = len(stages[0])

    def swap(x, bit, axis="wide"):
        size = lax.axis_size(axis)
        return lax.ppermute(x, axis, [(i, i ^ bit) for i in range(size)])

    slots = kept_slots[:, 0, 0]
    counts = kept_counts[:, 0, 0]
    live = jnp.arange(cap, dtype=jnp.int32)[None] < counts[:, None]
    is_down = jnp.arange(3)[:, None] == 2
    minor = jnp.where(is_down, row_blocks, HT)
    major_pos, minor_pos = slots // minor, slots % minor
    block = jnp.where(is_down, minor_pos, major_pos)
    column = jnp.where(live, jnp.where(is_down, major_pos, minor_pos), HT)
    idx = jnp.stack([block, column], axis=1)

    gate, up, down = pl.pallas_call(
        load_kernel,
        out_shape=[pltpu.VMEM((cap, tile, tile), BF16)] * 3,
        in_specs=[HBM] * 3,
        out_specs=[VM] * 3,
        scratch_shapes=[pltpu.SemaphoreType.DMA((3,))],
        compiler_params=pltpu.CompilerParams(vmem_limit_bytes=58 << 20),
        name="load",
    )(gate_tiles[0, 0], up_tiles[0, 0], down_tiles[0, 0])

    held = lax.optimization_barrier(jnp.stack([tokens, cotangent]))
    for stage in stages[::-1]:
        pieces = [held] + [swap(held, offset) for offset in stage[1:]]
        held = lax.optimization_barrier(jnp.concatenate(pieces, axis=1))
    panel = held

    parts = pl.pallas_call(
        functools.partial(forward_kernel, group),
        out_shape=pltpu.VMEM((3, HT, rows, tile), F32),
        in_specs=[SM, SM, VM, VM, VM, VM],
        out_specs=VM,
        compiler_params=VLIM,
        name="forward",
    )(idx, counts, panel, gate, up, down)

    narrow_bits = bits_of(n_narrow)
    for bit in narrow_bits[:-1]:
        parts = parts + swap(parts, bit, "narrow")
    other = swap(parts, narrow_bits[-1], "narrow")

    size = rows // quarters
    acts, keep, *sends = pl.pallas_call(
        functools.partial(backward_kernel, group, quarters),
        out_shape=[
            jax.ShapeDtypeStruct((3, HT + 1, rows, tile), BF16),
            jax.ShapeDtypeStruct((2, size, feats), F32),
        ]
        + [jax.ShapeDtypeStruct((2, size, feats), BF16)] * (quarters - 1),
        in_specs=[SM, SM] + [VM] * 5,
        out_specs=[VM] * (quarters + 1),
        scratch_shapes=[pltpu.VMEM((rows, feats), F32)] * 2,
        compiler_params=VLIM,
        name="backward",
    )(idx, counts, parts, other, gate, up, down)

    def tile_grads(m, which):
        return pl.pallas_call(
            functools.partial(grad_kernel, group, m, which),
            out_shape=jax.ShapeDtypeStruct((cap, tile, tile), BF16),
            in_specs=[SM, SM, VM, VM],
            out_specs=HBM,
            scratch_shapes=[
                pltpu.VMEM((cap, tile, tile), BF16),
                pltpu.SemaphoreType.DMA((cap // group,)),
            ],
            cost_estimate=pl.CostEstimate(
                flops=2 * cap * rows * tile * tile,
                bytes_accessed=4 * cap * tile * tile,
                transcendentals=0,
            ),
            compiler_params=VLIM,
        )(idx, counts, panel, acts)

    got = [swap(s, offset) for s, offset in zip(sends, stages[0][1:])]
    total = keep
    for g in got:
        total = total + g.astype(F32)
    for stage in stages[1:]:
        size = total.shape[1] // len(stage)
        pieces = [total[:, q * size:(q + 1) * size] for q in range(len(stage))]
        total = pieces[0]
        for piece, offset in zip(pieces[1:], stage[1:]):
            total = total + swap(piece.astype(BF16), offset).astype(F32)
    total = total.astype(BF16)
    grads = [tile_grads(m, w)[None, None] for m, w in ((0, 0), (1, 0), (2, 1))]
    return (total[0], total[1], *grads)


def solution(mesh):
    act = P("wide", "narrow")
    wts = P("narrow", "wide", None, None, None)
    in_specs = (act, act, wts, wts, wts, P(None, "narrow", "wide", None), P(None, "narrow", "wide"))
    out_specs = (act, act, wts, wts, wts)
    return jax.shard_map(
        per_device, mesh=mesh, in_specs=in_specs, out_specs=out_specs, check_vma=False
    )
```

profile of v0, /device:TPU:0, one launch (start us, length us, event | category | flops | bytes accessed | tf_op | source)
XLA Modules:
  0.0 47.6 jit_solution(15516797800084489805)
XLA Ops:
  0.6 0.8 %pad_maximum_fusion.2 = bf16[2,2,4096]{2,1,0:T(2,128)(2,1)S(1)} fusion(bf16[1,2,4096]{2,1,0:T(2,128)(2,1)} %bitcast.38, bf16[1,2,4096]{2,1,0:T(2,128)(2,1)} %bitcast.39), kind=kLoop, calls=%fused_computation.7 | loop fusion | flops 16384 | bytes 65536 | tf_op jit(solution)/shard_map/stack | solution.py:197
  1.4 5.1 %collective-permute-start.2 = (bf16[2,2,4096]{2,1,0:T(2,128)(2,1)S(1)}, bf16[2,2,4096]{2,1,0:T(2,128)(2,1)S(1)}, u32[]{:S(2)}, u32[]{:S(2)}) collective-permute-start(bf16[2,2,4096]{2,1,0:T(2,128)(2,1)S(1)} %pad_maximum_fusion.2), channel_id=1, source_target_pairs={{0,24},{2,26},{4,28},{6,30},{8,16},{10,18},{12,20},{14,22},{16,8},... | collective-permute-start | bytes 98312 | tf_op jit(solution)/shard_map/ppermute | solution.py:175
  6.6 0.0 collective-permute-start.1
  6.6 0.6 %collective-permute-start = (bf16[2,2,4096]{2,1,0:T(2,128)(2,1)S(1)}, bf16[2,2,4096]{2,1,0:T(2,128)(2,1)S(1)}, u32[]{:S(2)}, u32[]{:S(2)}) collective-permute-start(bf16[2,2,4096]{2,1,0:T(2,128)(2,1)S(1)} %pad_maximum_fusion.2), channel_id=1, source_target_pairs={{0,8},{2,10},{4,12},{6,14},{8,0},{10,2},{12,4},{14,6},{16,24},{18,... | collective-permute-start | bytes 98312 | tf_op jit(solution)/shard_map/ppermute | solution.py:175
  7.2 1.0 %broadcast_select_fusion.1 = (s32[3,1,48]{2,1,0:T(1,128)S(1)}, s32[3,1,48]{2,1,0:T(1,128)S(1)}, s32[3,1,48]{2,1,0:T(1,128)S(1)}) fusion(pred[3]{0:T(512)(128)(4,1)S(1)} %iota_compare_fusion, s32[3]{0:T(128)S(1)} %get-tuple-element.31, s32[3,1,1,48]{3,2,1,0:T(1,128)} %param.12, s32[3]{0:T(128)S(1)} %get-tuple-element.32, s32[3]{0:T(128)S(1)} %fusion.3), kind=kLoop, calls=%fused_computation.15 | loop fusion | flops 2160 | bytes 2343 | tf_op jit(solution)/shard_map/jit(_where)/select_n | solution.py:183
  8.2 0.2 collective-permute-done.2
  8.5 2.9 %collective-permute-done.1 = bf16[2,2,4096]{2,1,0:T(2,128)(2,1)S(1)} collective-permute-done((bf16[2,2,4096]{2,1,0:T(2,128)(2,1)S(1)}, bf16[2,2,4096]{2,1,0:T(2,128)(2,1)S(1)}, u32[]{:S(2)}, u32[]{:S(2)}) %collective-permute-start.1) | collective-permute-done | bytes 32800 | tf_op jit(solution)/shard_map/ppermute | solution.py:175
  11.4 0.0 collective-permute-done
  11.4 0.2 pad_maximum_fusion.1
  11.5 2.5 %collective-permute-start.5 = (bf16[2,8,4096]{2,1,0:T(8,128)(2,1)S(1)}, bf16[2,8,4096]{2,1,0:T(8,128)(2,1)S(1)}, u32[]{:S(2)}, u32[]{:S(2)}) collective-permute-start(bf16[2,8,4096]{2,1,0:T(8,128)(2,1)S(1)} %pad_maximum_fusion.1), channel_id=1, source_target_pairs={{0,6},{2,4},{4,2},{6,0},{8,14},{10,12},{12,10},{14,8},{16,22},{18,... | collective-permute-start | bytes 393224 | tf_op jit(solution)/shard_map/ppermute | solution.py:175
  14.0 0.5 %collective-permute-start.4 = (bf16[2,8,4096]{2,1,0:T(8,128)(2,1)S(1)}, bf16[2,8,4096]{2,1,0:T(8,128)(2,1)S(1)}, u32[]{:S(2)}, u32[]{:S(2)}) collective-permute-start(bf16[2,8,4096]{2,1,0:T(8,128)(2,1)S(1)} %pad_maximum_fusion.1), channel_id=1, source_target_pairs={{0,4},{2,6},{4,0},{6,2},{8,12},{10,14},{12,8},{14,10},{16,20},{18,... | collective-permute-start | bytes 393224 | tf_op jit(solution)/shard_map/ppermute | solution.py:175
  14.6 0.5 %collective-permute-start.3 = (bf16[2,8,4096]{2,1,0:T(8,128)(2,1)S(1)}, bf16[2,8,4096]{2,1,0:T(8,128)(2,1)S(1)}, u32[]{:S(2)}, u32[]{:S(2)}) collective-permute-start(bf16[2,8,4096]{2,1,0:T(8,128)(2,1)S(1)} %pad_maximum_fusion.1), channel_id=1, source_target_pairs={{0,2},{2,0},{4,6},{6,4},{8,10},{10,8},{12,14},{14,12},{16,18},{18,... | collective-permute-start | bytes 393224 | tf_op jit(solution)/shard_map/ppermute | solution.py:175
  15.1 0.7 %compare_select_fusion = s32[3,1,48]{2,1,0:T(1,128)S(1)} fusion(s32[3,1,48]{2,1,0:T(1,128)S(1)} %get-tuple-element.25, s32[3,1,48]{2,1,0:T(1,128)S(1)} %get-tuple-element.24, pred[3]{0:T(512)(128)(4,1)S(1)} %iota_compare_fusion, s32[3]{0:T(128)} %bitcast.26), kind=kLoop, calls=%fused_computation.10 | loop fusion | flops 432 | bytes 1743 | tf_op jit(solution)/shard_map/jit(_where)/select_n | solution.py:184
  15.8 0.0 copy-start
  15.8 2.4 %load.1 = (bf16[48,128,128]{2,1,0:T(8,128)(2,1)S(1)}, bf16[48,128,128]{2,1,0:T(8,128)(2,1)S(1)}, bf16[48,128,128]{2,1,0:T(8,128)(2,1)S(1)}) custom-call(bf16[48,128,128]{2,1,0:T(8,128)(2,1)} %bitcast.32, bf16[48,128,128]{2,1,0:T(8,128)(2,1)} %bitcast.33, bf16[48,128,128]{2,1,0:T(8,128)(2,1)} %bitcast.34), custom_call_target="tpu_custom_call" | custom-call | tf_op jit(solution)/shard_map/load/pallas_call | solution.py:187
  18.2 0.6 %collective-permute-done.5 = bf16[2,8,4096]{2,1,0:T(8,128)(2,1)S(1)} collective-permute-done((bf16[2,8,4096]{2,1,0:T(8,128)(2,1)S(1)}, bf16[2,8,4096]{2,1,0:T(8,128)(2,1)S(1)}, u32[]{:S(2)}, u32[]{:S(2)}) %collective-permute-start.5) | collective-permute-done | bytes 131104 | tf_op jit(solution)/shard_map/ppermute | solution.py:175
  18.9 0.8 %collective-permute-done.4 = bf16[2,8,4096]{2,1,0:T(8,128)(2,1)S(1)} collective-permute-done((bf16[2,8,4096]{2,1,0:T(8,128)(2,1)S(1)}, bf16[2,8,4096]{2,1,0:T(8,128)(2,1)S(1)}, u32[]{:S(2)}, u32[]{:S(2)}) %collective-permute-start.4) | collective-permute-done | bytes 131104 | tf_op jit(solution)/shard_map/ppermute | solution.py:175
  19.6 0.0 collective-permute-done.3
  19.7 0.0 copy-done
  19.7 2.5 %forward.1.parts = f32[3,3,32,128]{3,2,1,0:T(8,128)S(1)} custom-call(s32[3,2,48]{2,1,0:T(2,128)S(1)} %pad_add_fusion.idx, s32[3]{0:T(128)S(1)} %bitcast.27, bf16[2,32,4096]{2,1,0:T(8,128)(2,1)S(1)} %pad_maximum_fusion.panel, bf16[48,128,128]{2,1,0:T(8,128)(2,1)S(1)} %get-tuple-element.13.gate, bf16[48,128,128]{2,1,0:T(8,128)(2,1)S(1)} %get-tuple-element.14.up, ...), custom_call_target="tpu_custom_call" | custom-call | tf_op jit(solution)/shard_map/forward/pallas_call | solution.py:203
  22.2 0.1 collective-permute-start.6
  22.3 1.4 %collective-permute-done.6.other = f32[3,3,32,128]{3,2,1,0:T(8,128)S(1)} collective-permute-done((f32[3,3,32,128]{3,2,1,0:T(8,128)S(1)}, f32[3,3,32,128]{3,2,1,0:T(8,128)S(1)}, u32[]{:S(2)}, u32[]{:S(2)}) %collective-permute-start.6) | collective-permute-done | bytes 147488 | tf_op jit(solution)/shard_map/ppermute | solution.py:175
  23.7 2.8 %backward.1 = (bf16[3,4,32,128]{3,2,1,0:T(8,128)(2,1)S(1)}, f32[2,8,4096]{2,1,0:T(8,128)S(1)}, bf16[2,8,4096]{2,1,0:T(8,128)(2,1)S(1)}, bf16[2,8,4096]{2,1,0:T(8,128)(2,1)S(1)}, bf16[2,8,4096]{2,1,0:T(8,128)(2,1)S(1)}) custom-call(s32[3,2,48]{2,1,0:T(2,128)S(1)} %pad_add_fusion.idx, s32[3]{0:T(128)S(1)} %bitcast.28, f32[3,3,32,128]{3,2,1,0:T(8,128)S(1)} %forward.1.parts, ...), custom_call_target="tpu_custom_call" | custom-call | tf_op jit(solution)/shard_map/backward/pallas_call | solution.py:218
  26.5 1.1 %collective-permute-start.7 = (bf16[2,8,4096]{2,1,0:T(8,128)(2,1)S(1)}, bf16[2,8,4096]{2,1,0:T(8,128)(2,1)S(1)}, u32[]{:S(2)}, u32[]{:S(2)}) collective-permute-start(bf16[2,8,4096]{2,1,0:T(8,128)(2,1)S(1)} %get-tuple-element.17), channel_id=1, source_target_pairs={{0,2},{2,0},{4,6},{6,4},{8,10},{10,8},{12,14},{14,12},{16,18},{18,... | collective-permute-start | bytes 393224 | tf_op jit(solution)/shard_map/ppermute | solution.py:175
  27.6 2.2 %collective-permute-start.8 = (bf16[2,8,4096]{2,1,0:T(8,128)(2,1)S(1)}, bf16[2,8,4096]{2,1,0:T(8,128)(2,1)S(1)}, u32[]{:S(2)}, u32[]{:S(2)}) collective-permute-start(bf16[2,8,4096]{2,1,0:T(8,128)(2,1)S(1)} %get-tuple-element.18), channel_id=1, source_target_pairs={{0,4},{2,6},{4,0},{6,2},{8,12},{10,14},{12,8},{14,10},{16,20},{18,... | collective-permute-start | bytes 393224 | tf_op jit(solution)/shard_map/ppermute | solution.py:175
  29.8 0.5 %collective-permute-start.9 = (bf16[2,8,4096]{2,1,0:T(8,128)(2,1)S(1)}, bf16[2,8,4096]{2,1,0:T(8,128)(2,1)S(1)}, u32[]{:S(2)}, u32[]{:S(2)}) collective-permute-start(bf16[2,8,4096]{2,1,0:T(8,128)(2,1)S(1)} %get-tuple-element.19), channel_id=1, source_target_pairs={{0,6},{2,4},{4,2},{6,0},{8,14},{10,12},{12,10},{14,8},{16,22},{18,... | collective-permute-start | bytes 393224 | tf_op jit(solution)/shard_map/ppermute | solution.py:175
  30.4 1.8 %collective-permute-done.7 = bf16[2,8,4096]{2,1,0:T(8,128)(2,1)S(1)} collective-permute-done((bf16[2,8,4096]{2,1,0:T(8,128)(2,1)S(1)}, bf16[2,8,4096]{2,1,0:T(8,128)(2,1)S(1)}, u32[]{:S(2)}, u32[]{:S(2)}) %collective-permute-start.7) | collective-permute-done | bytes 131104 | tf_op jit(solution)/shard_map/ppermute | solution.py:175
  32.2 3.0 %collective-permute-done.8 = bf16[2,8,4096]{2,1,0:T(8,128)(2,1)S(1)} collective-permute-done((bf16[2,8,4096]{2,1,0:T(8,128)(2,1)S(1)}, bf16[2,8,4096]{2,1,0:T(8,128)(2,1)S(1)}, u32[]{:S(2)}, u32[]{:S(2)}) %collective-permute-start.8) | collective-permute-done | bytes 131104 | tf_op jit(solution)/shard_map/ppermute | solution.py:175
  35.2 1.8 %collective-permute-done.9 = bf16[2,8,4096]{2,1,0:T(8,128)(2,1)S(1)} collective-permute-done((bf16[2,8,4096]{2,1,0:T(8,128)(2,1)S(1)}, bf16[2,8,4096]{2,1,0:T(8,128)(2,1)S(1)}, u32[]{:S(2)}, u32[]{:S(2)}) %collective-permute-start.9) | collective-permute-done | bytes 131104 | tf_op jit(solution)/shard_map/ppermute | solution.py:175
  37.0 0.1 fusion.4
  37.1 0.1 fusion.5
  37.2 0.1 collective-permute-start.10
  37.3 2.2 %collective-permute-start.12 = (bf16[2,2,4096]{2,1,0:T(2,128)(2,1)S(1)}, bf16[2,2,4096]{2,1,0:T(2,128)(2,1)S(1)}, u32[]{:S(2)}, u32[]{:S(2)}) collective-permute-start(bf16[2,2,4096]{2,1,0:T(2,128)(2,1)S(1)} %get-tuple-element.27), channel_id=1, source_target_pairs={{0,24},{2,26},{4,28},{6,30},{8,16},{10,18},{12,20},{14,22},{16,8},... | collective-permute-start | bytes 98312 | tf_op jit(solution)/shard_map/ppermute | solution.py:175
  39.5 1.2 %collective-permute-start.11 = (bf16[2,2,4096]{2,1,0:T(2,128)(2,1)S(1)}, bf16[2,2,4096]{2,1,0:T(2,128)(2,1)S(1)}, u32[]{:S(2)}, u32[]{:S(2)}) collective-permute-start(bf16[2,2,4096]{2,1,0:T(2,128)(2,1)S(1)} %get-tuple-element.28), channel_id=1, source_target_pairs={{0,16},{2,18},{4,20},{6,22},{8,24},{10,26},{12,28},{14,30},{16,0},... | collective-permute-start | bytes 98312 | tf_op jit(solution)/shard_map/ppermute | solution.py:175
  40.7 2.0 %shard_map.112 = bf16[48,128,128]{2,1,0:T(8,128)(2,1)} custom-call(s32[3,2,48]{2,1,0:T(2,128)S(1)} %pad_add_fusion.idx, s32[3]{0:T(128)S(1)} %bitcast.29, bf16[2,32,4096]{2,1,0:T(8,128)(2,1)S(1)} %pad_maximum_fusion.panel, bf16[3,4,32,128]{3,2,1,0:T(8,128)(2,1)S(1)} %get-tuple-element.20.acts), custom_call_target="tpu_custom_call" | custom-call | flops 50331648 | bytes 3145728 | tf_op jit(solution)/shard_map/pallas_call | solution.py:233
  42.8 2.0 %shard_map.111 = bf16[48,128,128]{2,1,0:T(8,128)(2,1)} custom-call(s32[3,2,48]{2,1,0:T(2,128)S(1)} %pad_add_fusion.idx, s32[3]{0:T(128)S(1)} %bitcast.30, bf16[2,32,4096]{2,1,0:T(8,128)(2,1)S(1)} %pad_maximum_fusion.panel, bf16[3,4,32,128]{3,2,1,0:T(8,128)(2,1)S(1)} %get-tuple-element.20.acts), custom_call_target="tpu_custom_call" | custom-call | flops 50331648 | bytes 3145728 | tf_op jit(solution)/shard_map/pallas_call | solution.py:233
  44.8 2.0 %shard_map.110 = bf16[48,128,128]{2,1,0:T(8,128)(2,1)} custom-call(s32[3,2,48]{2,1,0:T(2,128)S(1)} %pad_add_fusion.idx, s32[3]{0:T(128)S(1)} %bitcast.31, bf16[2,32,4096]{2,1,0:T(8,128)(2,1)S(1)} %pad_maximum_fusion.panel, bf16[3,4,32,128]{3,2,1,0:T(8,128)(2,1)S(1)} %get-tuple-element.20.acts), custom_call_target="tpu_custom_call" | custom-call | flops 50331648 | bytes 3145728 | tf_op jit(solution)/shard_map/pallas_call | solution.py:233
  46.9 0.0 collective-permute-done.10
  46.9 0.0 collective-permute-done.12
  46.9 0.0 collective-permute-done.11
  46.9 0.1 fusion.2
  47.0 0.6 %slice_bitcast_fusion = (bf16[2,4096]{1,0:T(2,128)(2,1)}, bf16[2,4096]{1,0:T(2,128)(2,1)}) fusion(bf16[2,2,4096]{2,1,0:T(2,128)(2,1)S(1)} %fusion.2), kind=kLoop, calls=%fused_computation.8 | loop fusion | bytes 65536 | tf_op jit(solution)/shard_map/squeeze | solution.py:262
  (5 shorter events, 0.1 us)
Async XLA Ops:
  1.4 7.0 %collective-permute-start.2 = (bf16[2,2,4096]{2,1,0:T(2,128)(2,1)S(1)}, bf16[2,2,4096]{2,1,0:T(2,128)(2,1)S(1)}, u32[]{:S(2)}, u32[]{:S(2)}) collective-permute-start(bf16[2,2,4096]{2,1,0:T(2,128)(2,1)S(1)} %pad_maximum_fusion.2), channel_id=1, source_target_pairs={{0,24},{2,26},{4,28},{6,30},{8,16},{10,18},{12,20},{14,22},{16,8},... | collective-permute-start | bytes 98312 | tf_op jit(solution)/shard_map/ppermute | solution.py:175
  6.6 4.8 %collective-permute-start.1 = (bf16[2,2,4096]{2,1,0:T(2,128)(2,1)S(1)}, bf16[2,2,4096]{2,1,0:T(2,128)(2,1)S(1)}, u32[]{:S(2)}, u32[]{:S(2)}) collective-permute-start(bf16[2,2,4096]{2,1,0:T(2,128)(2,1)S(1)} %pad_maximum_fusion.2), channel_id=1, source_target_pairs={{0,16},{2,18},{4,20},{6,22},{8,24},{10,26},{12,28},{14,30},{16,0},... | collective-permute-start | bytes 98312 | tf_op jit(solution)/shard_map/ppermute | solution.py:175
  6.6 4.8 %collective-permute-start = (bf16[2,2,4096]{2,1,0:T(2,128)(2,1)S(1)}, bf16[2,2,4096]{2,1,0:T(2,128)(2,1)S(1)}, u32[]{:S(2)}, u32[]{:S(2)}) collective-permute-start(bf16[2,2,4096]{2,1,0:T(2,128)(2,1)S(1)} %pad_maximum_fusion.2), channel_id=1, source_target_pairs={{0,8},{2,10},{4,12},{6,14},{8,0},{10,2},{12,4},{14,6},{16,24},{18,... | collective-permute-start | bytes 98312 | tf_op jit(solution)/shard_map/ppermute | solution.py:175
  11.5 7.3 %collective-permute-start.5 = (bf16[2,8,4096]{2,1,0:T(8,128)(2,1)S(1)}, bf16[2,8,4096]{2,1,0:T(8,128)(2,1)S(1)}, u32[]{:S(2)}, u32[]{:S(2)}) collective-permute-start(bf16[2,8,4096]{2,1,0:T(8,128)(2,1)S(1)} %pad_maximum_fusion.1), channel_id=1, source_target_pairs={{0,6},{2,4},{4,2},{6,0},{8,14},{10,12},{12,10},{14,8},{16,22},{18,... | collective-permute-start | bytes 393224 | tf_op jit(solution)/shard_map/ppermute | solution.py:175
  14.0 5.6 %collective-permute-start.4 = (bf16[2,8,4096]{2,1,0:T(8,128)(2,1)S(1)}, bf16[2,8,4096]{2,1,0:T(8,128)(2,1)S(1)}, u32[]{:S(2)}, u32[]{:S(2)}) collective-permute-start(bf16[2,8,4096]{2,1,0:T(8,128)(2,1)S(1)} %pad_maximum_fusion.1), channel_id=1, source_target_pairs={{0,4},{2,6},{4,0},{6,2},{8,12},{10,14},{12,8},{14,10},{16,20},{18,... | collective-permute-start | bytes 393224 | tf_op jit(solution)/shard_map/ppermute | solution.py:175
  14.6 5.1 %collective-permute-start.3 = (bf16[2,8,4096]{2,1,0:T(8,128)(2,1)S(1)}, bf16[2,8,4096]{2,1,0:T(8,128)(2,1)S(1)}, u32[]{:S(2)}, u32[]{:S(2)}) collective-permute-start(bf16[2,8,4096]{2,1,0:T(8,128)(2,1)S(1)} %pad_maximum_fusion.1), channel_id=1, source_target_pairs={{0,2},{2,0},{4,6},{6,4},{8,10},{10,8},{12,14},{14,12},{16,18},{18,... | collective-permute-start | bytes 393224 | tf_op jit(solution)/shard_map/ppermute | solution.py:175
  15.8 3.9 %copy-start = (s32[3,1,1]{0,2,1:T(1,128)S(1)}, s32[3,1,1]{0,2,1:T(1,128)}, u32[]{:S(2)}) copy-start(s32[3,1,1]{0,2,1:T(1,128)} %param.13) | copy-start | bytes 40
  22.2 1.4 %collective-permute-start.6 = (f32[3,3,32,128]{3,2,1,0:T(8,128)S(1)}, f32[3,3,32,128]{3,2,1,0:T(8,128)S(1)}, u32[]{:S(2)}, u32[]{:S(2)}) collective-permute-start(f32[3,3,32,128]{3,2,1,0:T(8,128)S(1)} %forward.1.parts), channel_id=1, source_target_pairs={{0,1},{1,0},{2,3},{3,2},{4,5},{5,4},{6,7},{7,6},{8,9},{9,8},{10,11... | collective-permute-start | bytes 442376 | tf_op jit(solution)/shard_map/ppermute | solution.py:175
  26.5 5.7 %collective-permute-start.7 = (bf16[2,8,4096]{2,1,0:T(8,128)(2,1)S(1)}, bf16[2,8,4096]{2,1,0:T(8,128)(2,1)S(1)}, u32[]{:S(2)}, u32[]{:S(2)}) collective-permute-start(bf16[2,8,4096]{2,1,0:T(8,128)(2,1)S(1)} %get-tuple-element.17), channel_id=1, source_target_pairs={{0,2},{2,0},{4,6},{6,4},{8,10},{10,8},{12,14},{14,12},{16,18},{18,... | collective-permute-start | bytes 393224 | tf_op jit(solution)/shard_map/ppermute | solution.py:175
  27.6 7.5 %collective-permute-start.8 = (bf16[2,8,4096]{2,1,0:T(8,128)(2,1)S(1)}, bf16[2,8,4096]{2,1,0:T(8,128)(2,1)S(1)}, u32[]{:S(2)}, u32[]{:S(2)}) collective-permute-start(bf16[2,8,4096]{2,1,0:T(8,128)(2,1)S(1)} %get-tuple-element.18), channel_id=1, source_target_pairs={{0,4},{2,6},{4,0},{6,2},{8,12},{10,14},{12,8},{14,10},{16,20},{18,... | collective-permute-start | bytes 393224 | tf_op jit(solution)/shard_map/ppermute | solution.py:175
  29.8 7.2 %collective-permute-start.9 = (bf16[2,8,4096]{2,1,0:T(8,128)(2,1)S(1)}, bf16[2,8,4096]{2,1,0:T(8,128)(2,1)S(1)}, u32[]{:S(2)}, u32[]{:S(2)}) collective-permute-start(bf16[2,8,4096]{2,1,0:T(8,128)(2,1)S(1)} %get-tuple-element.19), channel_id=1, source_target_pairs={{0,6},{2,4},{4,2},{6,0},{8,14},{10,12},{12,10},{14,8},{16,22},{18,... | collective-permute-start | bytes 393224 | tf_op jit(solution)/shard_map/ppermute | solution.py:175
  37.2 9.7 %collective-permute-start.10 = (bf16[2,2,4096]{2,1,0:T(2,128)(2,1)S(1)}, bf16[2,2,4096]{2,1,0:T(2,128)(2,1)S(1)}, u32[]{:S(2)}, u32[]{:S(2)}) collective-permute-start(bf16[2,2,4096]{2,1,0:T(2,128)(2,1)S(1)} %get-tuple-element.26), channel_id=1, source_target_pairs={{0,8},{2,10},{4,12},{6,14},{8,0},{10,2},{12,4},{14,6},{16,24},{18,... | collective-permute-start | bytes 98312 | tf_op jit(solution)/shard_map/ppermute | solution.py:175
  37.3 9.6 %collective-permute-start.12 = (bf16[2,2,4096]{2,1,0:T(2,128)(2,1)S(1)}, bf16[2,2,4096]{2,1,0:T(2,128)(2,1)S(1)}, u32[]{:S(2)}, u32[]{:S(2)}) collective-permute-start(bf16[2,2,4096]{2,1,0:T(2,128)(2,1)S(1)} %get-tuple-element.27), channel_id=1, source_target_pairs={{0,24},{2,26},{4,28},{6,30},{8,16},{10,18},{12,20},{14,22},{16,8},... | collective-permute-start | bytes 98312 | tf_op jit(solution)/shard_map/ppermute | solution.py:175
  39.5 7.4 %collective-permute-start.11 = (bf16[2,2,4096]{2,1,0:T(2,128)(2,1)S(1)}, bf16[2,2,4096]{2,1,0:T(2,128)(2,1)S(1)}, u32[]{:S(2)}, u32[]{:S(2)}) collective-permute-start(bf16[2,2,4096]{2,1,0:T(2,128)(2,1)S(1)} %get-tuple-element.28), channel_id=1, source_target_pairs={{0,16},{2,18},{4,20},{6,22},{8,24},{10,26},{12,28},{14,30},{16,0},... | collective-permute-start | bytes 98312 | tf_op jit(solution)/shard_map/ppermute | solution.py:175
where the time goes:
time: 48 us; the launch traced here: 47.6 us
  starting transfers between devices  16.8 us (35%)
  Pallas kernels  13.9 us (29%)
  waiting for transfers between devices  12.6 us (26%)
  other arithmetic  2.88 us (6%)
  between operations  0.78 us (2%)
  local copies, waits for them, and re-layouts  0.73 us (2%)
    ppermute x13, starting transfers between devices, swap(): return lax.ppermute(x, axis, [(i, i ^ bit) for i in range(size)])  16.8 us
    ppermute x13, waiting for transfers between devices, swap(): return lax.ppermute(x, axis, [(i, i ^ bit) for i in range(size)])  12.6 us
    pallas_call x3, Pallas kernels, tile_grads(): pl.pallas_call(functools.partial(grad_kernel, group, m, which), out_shape...  6.13 us
    pallas_call x1, Pallas kernels, per_device(): pl.pallas_call(functools.partial(backward_kernel, group, quarters), out_s...  2.84 us
    pallas_call x1, Pallas kernels, per_device(): pl.pallas_call(functools.partial(forward_kernel, group), out_shape=pltpu....  2.53 us
    pallas_call x1, Pallas kernels, per_device(): pl.pallas_call(load_kernel, out_shape=[pltpu.VMEM((cap, tile, tile), BF16...  2.39 us
    select_n x1, other arithmetic, per_device(): block = jnp.where(is_down, minor_pos, major_pos)  1.02 us
  transfers between devices with their start and end apart: 13, of which 8 were waited for; matrix products, arithmetic and copies ran while one was open for 4% of the time, Pallas kernels for 18%

commit v1 on v0

--- a/solution.py
+++ b/solution.py
@@ -18,7 +18,7 @@
 
 
 def group_of(cap):
-    for size in (8, 6, 4, 3, 2):
+    for size in (8, 6, 4, 2):
         if cap % size == 0:
             return size
     return 1
@@ -28,50 +28,44 @@
     return pl.ds(pl.multiple_of(index * tile, tile), tile)
 
 
-def live_groups(count, group):
-    return lax.div(count + (group - 1), group)
-
-
-def forward_kernel(group, idx, counts, panel, gate, up, down, parts):
+def forward_kernel(group, idx, panel, gate, up, down, parts):
     tile = gate.shape[-1]
     rows = panel.shape[1]
 
     def stacked(which, m, base):
-        blocks = []
+        stack = []
         for j in range(group):
             k = base + j
             block = idx[m, 0, k]
             col = idx[m, 1, k]
             pick = panel[which, :, lanes(block, tile)]
             zero = jnp.zeros_like(pick)
-            blocks.append(
+            stack.append(
                 jnp.concatenate([jnp.where(col == c, pick, zero) for c in range(HT)], axis=0)
             )
-        return jnp.concatenate(blocks, axis=1)
-
-    for m, which, ref in ((0, 0, gate), (1, 0, up), (2, 1, down)):
-
-        def step(g, acc, m=m, which=which, ref=ref):
-            base = g * group
-            lhs = stacked(which, m, base)
-            if m < 2:
-                rhs = ref[pl.ds(base, group)].reshape(group * tile, tile)
-                return acc + lax.dot_general(
-                    lhs, rhs, (((1,), (0,)), ((), ())), preferred_element_type=F32
-                )
+        return jnp.concatenate(stack, axis=1)
+
+    def one(g, m, which, ref):
+        base = g * group
+        lhs = stacked(which, m, base)
+        if m < 2:
+            rhs = ref[pl.ds(base, group)].reshape(group * tile, tile)
+            dims = (((1,), (0,)), ((), ()))
+        else:
             rhs = jnp.concatenate([ref[base + j] for j in range(group)], axis=1)
-            return acc + lax.dot_general(
-                lhs, rhs, (((1,), (1,)), ((), ())), preferred_element_type=F32
-            )
-
-        total = lax.fori_loop(
-            0, live_groups(counts[m], group), step, jnp.zeros((HT * rows, tile), F32)
-        )
-        parts[m] = total.reshape(HT, rows, tile)
+            dims = (((1,), (1,)), ((), ()))
+        return lax.dot_general(lhs, rhs, dims, preferred_element_type=F32)
+
+    totals = [jnp.zeros((HT * rows, tile), F32)] * 3
+    for g in range(gate.shape[0] // group):
+        for m, which, ref in ((0, 0, gate), (1, 0, up), (2, 1, down)):
+            totals[m] = totals[m] + one(g, m, which, ref)
+    for m in range(3):
+        parts[m] = totals[m].reshape(HT, rows, tile)
 
 
 def backward_kernel(
-    group, quarters, idx, counts, parts, other, gate, up, down, acts, keep, *rest
+    group, quarters, idx, parts, other, gate, up, down, acts, keep, *rest
 ):
     sends, (out_sum, in_sum) = rest[:quarters - 1], rest[quarters - 1:]
     tile = gate.shape[-1]
@@ -89,23 +83,32 @@
         acts[m, HT] = jnp.zeros((rows, tile), BF16)
     out_sum[...] = jnp.zeros_like(out_sum)
     in_sum[...] = jnp.zeros_like(in_sum)
-    for m, ref, target in ((2, down, out_sum), (0, gate, in_sum), (1, up, in_sum)):
-
-        def step(g, carry, m=m, ref=ref, target=target):
-            base = g * group
+    blank = jnp.zeros((rows, tile), BF16)
+    for g in range(gate.shape[0] // group):
+        base = g * group
+        for m, ref, target in ((2, down, out_sum), (0, gate, in_sum), (1, up, in_sum)):
             products = []
-            for j in range(group):
-                lhs = acts[m, idx[m, 1, base + j]]
-                dims = (((1,), (0 if m == 2 else 1,)), ((), ()))
-                products.append(
-                    lax.dot_general(lhs, ref[base + j], dims, preferred_element_type=F32)
+            for j in range(0, group, 2):
+                k = base + j
+                first, second = acts[m, idx[m, 1, k]], acts[m, idx[m, 1, k + 1]]
+                lhs = jnp.concatenate(
+                    [
+                        jnp.concatenate([first, blank], axis=1),
+                        jnp.concatenate([blank, second], axis=1),
+                    ],
+                    axis=0,
                 )
+                if m == 2:
+                    rhs = ref[pl.ds(k, 2)].reshape(2 * tile, tile)
+                    dims = (((1,), (0,)), ((), ()))
+                else:
+                    rhs = jnp.concatenate([ref[k], ref[k + 1]], axis=1)
+                    dims = (((1,), (1,)), ((), ()))
+                both = lax.dot_general(lhs, rhs, dims, preferred_element_type=F32)
+                products += [both[:rows], both[rows:]]
             for j in range(group):
                 where = lanes(idx[m, 0, base + j], tile)
                 target[:, where] += products[j]
-            return carry
-
-        lax.fori_loop(0, live_groups(counts[m], group), step, 0)
     size = rows // quarters
     for which, total in ((0, out_sum), (1, in_sum)):
         keep[which] = total[:size]
@@ -113,24 +116,24 @@
             sends[q - 1][which] = total[q * size:(q + 1) * size].astype(BF16)
 
 
-def grad_kernel(group, m, which, idx, counts, panel, acts, out, buf, sem):
-    tile = out.shape[-1]
-    cap = out.shape[0]
+def grad_kernel(group, jobs, idx, panel, acts, *refs):
+    outs, bufs, sem = refs[:len(jobs)], refs[len(jobs):-1], refs[-1]
+    tile = outs[0].shape[-1]
+    cap = outs[0].shape[0]
     copies = []
-    for g in range(cap // group):
-        for j in range(group):
-            k = g * group + j
-            block = panel[which, :, lanes(idx[m, 0, k], tile)]
-            act = acts[m, idx[m, 1, k]]
-            left, right = (act, block) if m == 2 else (block, act)
-            buf[k] = lax.dot_general(
-                left, right, (((0,), (0,)), ((), ())), preferred_element_type=F32
-            ).astype(BF16)
-        copy = pltpu.make_async_copy(
-            buf.at[pl.ds(g * group, group)], out.at[pl.ds(g * group, group)], sem.at[g]
-        )
-        copy.start()
-        copies.append(copy)
+    for i, (m, which) in enumerate(jobs):
+        for g in range(cap // group):
+            for k in range(g * group, (g + 1) * group):
+                block = panel[which, :, lanes(idx[m, 0, k], tile)]
+                act = acts[m, idx[m, 1, k]]
+                left, right = (act, block) if m == 2 else (block, act)
+                bufs[i][k] = lax.dot_general(
+                    left, right, (((0,), (0,)), ((), ())), preferred_element_type=F32
+                ).astype(BF16)
+            span = pl.ds(g * group, group)
+            copy = pltpu.make_async_copy(bufs[i].at[span], outs[i].at[span], sem.at[i, g])
+            copy.start()
+            copies.append(copy)
     for copy in copies:
         copy.wait()
 
@@ -203,11 +206,11 @@
     parts = pl.pallas_call(
         functools.partial(forward_kernel, group),
         out_shape=pltpu.VMEM((3, HT, rows, tile), F32),
-        in_specs=[SM, SM, VM, VM, VM, VM],
+        in_specs=[SM, VM, VM, VM, VM],
         out_specs=VM,
         compiler_params=VLIM,
         name="forward",
-    )(idx, counts, panel, gate, up, down)
+    )(idx, panel, gate, up, down)
 
     narrow_bits = bits_of(n_narrow)
     for bit in narrow_bits[:-1]:
@@ -222,30 +225,28 @@
             jax.ShapeDtypeStruct((2, size, feats), F32),
         ]
         + [jax.ShapeDtypeStruct((2, size, feats), BF16)] * (quarters - 1),
-        in_specs=[SM, SM] + [VM] * 5,
+        in_specs=[SM] + [VM] * 5,
         out_specs=[VM] * (quarters + 1),
         scratch_shapes=[pltpu.VMEM((rows, feats), F32)] * 2,
         compiler_params=VLIM,
         name="backward",
-    )(idx, counts, parts, other, gate, up, down)
-
-    def tile_grads(m, which):
+    )(idx, parts, other, gate, up, down)
+
+    def tile_grads(jobs):
         return pl.pallas_call(
-            functools.partial(grad_kernel, group, m, which),
-            out_shape=jax.ShapeDtypeStruct((cap, tile, tile), BF16),
-            in_specs=[SM, SM, VM, VM],
-            out_specs=HBM,
-            scratch_shapes=[
-                pltpu.VMEM((cap, tile, tile), BF16),
-                pltpu.SemaphoreType.DMA((cap // group,)),
-            ],
+            functools.partial(grad_kernel, group, jobs),
+            out_shape=[jax.ShapeDtypeStruct((cap, tile, tile), BF16)] * len(jobs),
+            in_specs=[SM, VM, VM],
+            out_specs=[HBM] * len(jobs),
+            scratch_shapes=[pltpu.VMEM((cap, tile, tile), BF16)] * len(jobs)
+            + [pltpu.SemaphoreType.DMA((len(jobs), cap // group))],
             cost_estimate=pl.CostEstimate(
-                flops=2 * cap * rows * tile * tile,
-                bytes_accessed=4 * cap * tile * tile,
+                flops=len(jobs) * 2 * cap * rows * tile * tile,
+                bytes_accessed=len(jobs) * 4 * cap * tile * tile,
                 transcendentals=0,
             ),
             compiler_params=VLIM,
-        )(idx, counts, panel, acts)
+        )(idx, panel, acts)
 
     got = [swap(s, offset) for s, offset in zip(sends, stages[0][1:])]
     total = keep
@@ -258,7 +259,8 @@
         for piece, offset in zip(pieces[1:], stage[1:]):
             total = total + swap(piece.astype(BF16), offset).astype(F32)
     total = total.astype(BF16)
-    grads = [tile_grads(m, w)[None, None] for m, w in ((0, 0), (1, 0), (2, 1))]
+    gate_grad, up_grad, down_grad = tile_grads(((0, 0), (1, 0), (2, 1)))
+    grads = [g[None, None] for g in (gate_grad, up_grad, down_grad)]
     return (total[0], total[1], *grads)
 
 

time: 48 us -> 44 us (0.917)
  Pallas kernels: 13.9 us -> 9.58 us
  waiting for transfers between devices: 12.6 us -> 13.2 us
    pallas_call x3 -> x1, Pallas kernels: 6.13 us -> 3.17 us  [tile_grads(): pl.pallas_call(functools.partial(grad_kernel, group, jobs), out_shape=[ja...]
    pallas_call x1, Pallas kernels: 2.53 us -> 1.84 us  [per_device(): pl.pallas_call(functools.partial(forward_kernel, group), out_shape=pltpu....]
    ppermute x13, waiting for transfers between devices: 12.6 us -> 13.2 us  [swap(): return lax.ppermute(x, axis, [(i, i ^ bit) for i in range(size)])]
    pallas_call x1, Pallas kernels: 2.84 us -> 2.18 us  [per_device(): pl.pallas_call(functools.partial(backward_kernel, group, quarters), out_s...]
  transfers between devices with their start and end apart: 13 -> 13, of which waited for: 8 -> 9; matrix products, arithmetic and copies ran while one was open for 4% -> 4% of each run, Pallas kernels for 18% -> 13%
where the time goes in v1:
time: 44 us; the launch traced here: 43.7 us
  starting transfers between devices  16.5 us (38%)
  waiting for transfers between devices  13.2 us (30%)
  Pallas kernels  9.58 us (22%)
  other arithmetic  2.87 us (7%)
  between operations  0.74 us (2%)
  local copies, waits for them, and re-layouts  0.73 us (2%)
    ppermute x13, starting transfers between devices, swap(): return lax.ppermute(x, axis, [(i, i ^ bit) for i in range(size)])  16.5 us
    ppermute x13, waiting for transfers between devices, swap(): return lax.ppermute(x, axis, [(i, i ^ bit) for i in range(size)])  13.2 us
    pallas_call x1, Pallas kernels, tile_grads(): pl.pallas_call(functools.partial(grad_kernel, group, jobs), out_shape=[ja...  3.17 us
    pallas_call x1, Pallas kernels, per_device(): pl.pallas_call(load_kernel, out_shape=[pltpu.VMEM((cap, tile, tile), BF16...  2.38 us
    pallas_call x1, Pallas kernels, per_device(): pl.pallas_call(functools.partial(backward_kernel, group, quarters), out_s...  2.18 us
    pallas_call x1, Pallas kernels, per_device(): pl.pallas_call(functools.partial(forward_kernel, group), out_shape=pltpu....  1.84 us
    select_n x1, other arithmetic, per_device(): block = jnp.where(is_down, minor_pos, major_pos)  1.02 us
  transfers between devices with their start and end apart: 13, of which 9 were waited for; matrix products, arithmetic and copies ran while one was open for 4% of the time, Pallas kernels for 13%

profile of v1, /device:TPU:0, one launch (start us, length us, event | category | flops | bytes accessed | tf_op | source)
XLA Modules:
  0.0 43.7 jit_solution(17789302602179546551)
XLA Ops:
  0.6 0.8 %pad_maximum_fusion.2 = bf16[2,2,4096]{2,1,0:T(2,128)(2,1)S(1)} fusion(bf16[1,2,4096]{2,1,0:T(2,128)(2,1)} %bitcast.29, bf16[1,2,4096]{2,1,0:T(2,128)(2,1)} %bitcast.30), kind=kLoop, calls=%fused_computation.7 | loop fusion | flops 16384 | bytes 65536 | tf_op jit(solution)/shard_map/stack | solution.py:200
  1.4 5.1 %collective-permute-start.2 = (bf16[2,2,4096]{2,1,0:T(2,128)(2,1)S(1)}, bf16[2,2,4096]{2,1,0:T(2,128)(2,1)S(1)}, u32[]{:S(2)}, u32[]{:S(2)}) collective-permute-start(bf16[2,2,4096]{2,1,0:T(2,128)(2,1)S(1)} %pad_maximum_fusion.2), channel_id=1, source_target_pairs={{0,24},{2,26},{4,28},{6,30},{8,16},{10,18},{12,20},{14,22},{16,8},... | collective-permute-start | bytes 98312 | tf_op jit(solution)/shard_map/ppermute | solution.py:178
  6.6 0.0 collective-permute-start.1
  6.6 0.6 %collective-permute-start = (bf16[2,2,4096]{2,1,0:T(2,128)(2,1)S(1)}, bf16[2,2,4096]{2,1,0:T(2,128)(2,1)S(1)}, u32[]{:S(2)}, u32[]{:S(2)}) collective-permute-start(bf16[2,2,4096]{2,1,0:T(2,128)(2,1)S(1)} %pad_maximum_fusion.2), channel_id=1, source_target_pairs={{0,8},{2,10},{4,12},{6,14},{8,0},{10,2},{12,4},{14,6},{16,24},{18,... | collective-permute-start | bytes 98312 | tf_op jit(solution)/shard_map/ppermute | solution.py:178
  7.2 1.0 %broadcast_select_fusion.1 = (s32[3,1,48]{2,1,0:T(1,128)S(1)}, s32[3,1,48]{2,1,0:T(1,128)S(1)}, s32[3,1,48]{2,1,0:T(1,128)S(1)}) fusion(pred[3]{0:T(512)(128)(4,1)S(1)} %iota_compare_fusion, s32[3]{0:T(128)S(1)} %get-tuple-element.37, s32[3,1,1,48]{3,2,1,0:T(1,128)} %param.12, s32[3]{0:T(128)S(1)} %get-tuple-element.38, s32[3]{0:T(128)S(1)} %fusion.3), kind=kLoop, calls=%fused_computation.15 | loop fusion | flops 2160 | bytes 2343 | tf_op jit(solution)/shard_map/jit(_where)/select_n | solution.py:186
  8.2 0.2 collective-permute-done.2
  8.5 2.9 %collective-permute-done.1 = bf16[2,2,4096]{2,1,0:T(2,128)(2,1)S(1)} collective-permute-done((bf16[2,2,4096]{2,1,0:T(2,128)(2,1)S(1)}, bf16[2,2,4096]{2,1,0:T(2,128)(2,1)S(1)}, u32[]{:S(2)}, u32[]{:S(2)}) %collective-permute-start.1) | collective-permute-done | bytes 32800 | tf_op jit(solution)/shard_map/ppermute | solution.py:178
  11.4 0.0 collective-permute-done
  11.4 0.2 pad_maximum_fusion.1
  11.5 2.5 %collective-permute-start.5 = (bf16[2,8,4096]{2,1,0:T(8,128)(2,1)S(1)}, bf16[2,8,4096]{2,1,0:T(8,128)(2,1)S(1)}, u32[]{:S(2)}, u32[]{:S(2)}) collective-permute-start(bf16[2,8,4096]{2,1,0:T(8,128)(2,1)S(1)} %pad_maximum_fusion.1), channel_id=1, source_target_pairs={{0,6},{2,4},{4,2},{6,0},{8,14},{10,12},{12,10},{14,8},{16,22},{18,... | collective-permute-start | bytes 393224 | tf_op jit(solution)/shard_map/ppermute | solution.py:178
  14.0 0.5 %collective-permute-start.4 = (bf16[2,8,4096]{2,1,0:T(8,128)(2,1)S(1)}, bf16[2,8,4096]{2,1,0:T(8,128)(2,1)S(1)}, u32[]{:S(2)}, u32[]{:S(2)}) collective-permute-start(bf16[2,8,4096]{2,1,0:T(8,128)(2,1)S(1)} %pad_maximum_fusion.1), channel_id=1, source_target_pairs={{0,4},{2,6},{4,0},{6,2},{8,12},{10,14},{12,8},{14,10},{16,20},{18,... | collective-permute-start | bytes 393224 | tf_op jit(solution)/shard_map/ppermute | solution.py:178
  14.6 0.5 %collective-permute-start.3 = (bf16[2,8,4096]{2,1,0:T(8,128)(2,1)S(1)}, bf16[2,8,4096]{2,1,0:T(8,128)(2,1)S(1)}, u32[]{:S(2)}, u32[]{:S(2)}) collective-permute-start(bf16[2,8,4096]{2,1,0:T(8,128)(2,1)S(1)} %pad_maximum_fusion.1), channel_id=1, source_target_pairs={{0,2},{2,0},{4,6},{6,4},{8,10},{10,8},{12,14},{14,12},{16,18},{18,... | collective-permute-start | bytes 393224 | tf_op jit(solution)/shard_map/ppermute | solution.py:178
  15.1 0.7 %compare_select_fusion = s32[3,1,48]{2,1,0:T(1,128)S(1)} fusion(s32[3,1,48]{2,1,0:T(1,128)S(1)} %get-tuple-element.31, s32[3,1,48]{2,1,0:T(1,128)S(1)} %get-tuple-element.30, pred[3]{0:T(512)(128)(4,1)S(1)} %iota_compare_fusion, s32[3]{0:T(128)} %bitcast.31), kind=kLoop, calls=%fused_computation.10 | loop fusion | flops 432 | bytes 1743 | tf_op jit(solution)/shard_map/jit(_where)/select_n | solution.py:187
  15.8 2.4 %load.1 = (bf16[48,128,128]{2,1,0:T(8,128)(2,1)S(1)}, bf16[48,128,128]{2,1,0:T(8,128)(2,1)S(1)}, bf16[48,128,128]{2,1,0:T(8,128)(2,1)S(1)}) custom-call(bf16[48,128,128]{2,1,0:T(8,128)(2,1)} %bitcast.26, bf16[48,128,128]{2,1,0:T(8,128)(2,1)} %bitcast.27, bf16[48,128,128]{2,1,0:T(8,128)(2,1)} %bitcast.28), custom_call_target="tpu_custom_call" | custom-call | tf_op jit(solution)/shard_map/load/pallas_call | solution.py:190
  18.2 0.6 %collective-permute-done.5 = bf16[2,8,4096]{2,1,0:T(8,128)(2,1)S(1)} collective-permute-done((bf16[2,8,4096]{2,1,0:T(8,128)(2,1)S(1)}, bf16[2,8,4096]{2,1,0:T(8,128)(2,1)S(1)}, u32[]{:S(2)}, u32[]{:S(2)}) %collective-permute-start.5) | collective-permute-done | bytes 131104 | tf_op jit(solution)/shard_map/ppermute | solution.py:178
  18.9 0.8 %collective-permute-done.4 = bf16[2,8,4096]{2,1,0:T(8,128)(2,1)S(1)} collective-permute-done((bf16[2,8,4096]{2,1,0:T(8,128)(2,1)S(1)}, bf16[2,8,4096]{2,1,0:T(8,128)(2,1)S(1)}, u32[]{:S(2)}, u32[]{:S(2)}) %collective-permute-start.4) | collective-permute-done | bytes 131104 | tf_op jit(solution)/shard_map/ppermute | solution.py:178
  19.6 0.0 collective-permute-done.3
  19.7 1.8 %forward.1.parts = f32[3,3,32,128]{3,2,1,0:T(8,128)S(1)} custom-call(s32[3,2,48]{2,1,0:T(2,128)S(1)} %pad_add_fusion.idx, bf16[2,32,4096]{2,1,0:T(8,128)(2,1)S(1)} %pad_maximum_fusion.panel, bf16[48,128,128]{2,1,0:T(8,128)(2,1)S(1)} %get-tuple-element.16.gate, bf16[48,128,128]{2,1,0:T(8,128)(2,1)S(1)} %get-tuple-element.17.up, ...), custom_call_target="tpu_custom_call" | custom-call | tf_op jit(solution)/shard_map/forward/pallas_call | solution.py:206
  21.5 0.1 collective-permute-start.6
  21.6 1.4 %collective-permute-done.6.other = f32[3,3,32,128]{3,2,1,0:T(8,128)S(1)} collective-permute-done((f32[3,3,32,128]{3,2,1,0:T(8,128)S(1)}, f32[3,3,32,128]{3,2,1,0:T(8,128)S(1)}, u32[]{:S(2)}, u32[]{:S(2)}) %collective-permute-start.6) | collective-permute-done | bytes 147488 | tf_op jit(solution)/shard_map/ppermute | solution.py:178
  23.0 2.2 %backward.1 = (bf16[3,4,32,128]{3,2,1,0:T(8,128)(2,1)S(1)}, f32[2,8,4096]{2,1,0:T(8,128)S(1)}, bf16[2,8,4096]{2,1,0:T(8,128)(2,1)S(1)}, bf16[2,8,4096]{2,1,0:T(8,128)(2,1)S(1)}, bf16[2,8,4096]{2,1,0:T(8,128)(2,1)S(1)}) custom-call(s32[3,2,48]{2,1,0:T(2,128)S(1)} %pad_add_fusion.idx, f32[3,3,32,128]{3,2,1,0:T(8,128)S(1)} %forward.1.parts, ...), custom_call_target="tpu_custom_call" | custom-call | tf_op jit(solution)/shard_map/backward/pallas_call | solution.py:221
  25.2 1.2 %collective-permute-start.7 = (bf16[2,8,4096]{2,1,0:T(8,128)(2,1)S(1)}, bf16[2,8,4096]{2,1,0:T(8,128)(2,1)S(1)}, u32[]{:S(2)}, u32[]{:S(2)}) collective-permute-start(bf16[2,8,4096]{2,1,0:T(8,128)(2,1)S(1)} %get-tuple-element.20), channel_id=1, source_target_pairs={{0,2},{2,0},{4,6},{6,4},{8,10},{10,8},{12,14},{14,12},{16,18},{18,... | collective-permute-start | bytes 393224 | tf_op jit(solution)/shard_map/ppermute | solution.py:178
  26.3 0.8 %collective-permute-start.8 = (bf16[2,8,4096]{2,1,0:T(8,128)(2,1)S(1)}, bf16[2,8,4096]{2,1,0:T(8,128)(2,1)S(1)}, u32[]{:S(2)}, u32[]{:S(2)}) collective-permute-start(bf16[2,8,4096]{2,1,0:T(8,128)(2,1)S(1)} %get-tuple-element.21), channel_id=1, source_target_pairs={{0,4},{2,6},{4,0},{6,2},{8,12},{10,14},{12,8},{14,10},{16,20},{18,... | collective-permute-start | bytes 393224 | tf_op jit(solution)/shard_map/ppermute | solution.py:178
  27.1 1.6 %collective-permute-start.9 = (bf16[2,8,4096]{2,1,0:T(8,128)(2,1)S(1)}, bf16[2,8,4096]{2,1,0:T(8,128)(2,1)S(1)}, u32[]{:S(2)}, u32[]{:S(2)}) collective-permute-start(bf16[2,8,4096]{2,1,0:T(8,128)(2,1)S(1)} %get-tuple-element.22), channel_id=1, source_target_pairs={{0,6},{2,4},{4,2},{6,0},{8,14},{10,12},{12,10},{14,8},{16,22},{18,... | collective-permute-start | bytes 393224 | tf_op jit(solution)/shard_map/ppermute | solution.py:178
  28.7 2.8 %collective-permute-done.7 = bf16[2,8,4096]{2,1,0:T(8,128)(2,1)S(1)} collective-permute-done((bf16[2,8,4096]{2,1,0:T(8,128)(2,1)S(1)}, bf16[2,8,4096]{2,1,0:T(8,128)(2,1)S(1)}, u32[]{:S(2)}, u32[]{:S(2)}) %collective-permute-start.7) | collective-permute-done | bytes 131104 | tf_op jit(solution)/shard_map/ppermute | solution.py:178
  31.6 0.9 %collective-permute-done.8 = bf16[2,8,4096]{2,1,0:T(8,128)(2,1)S(1)} collective-permute-done((bf16[2,8,4096]{2,1,0:T(8,128)(2,1)S(1)}, bf16[2,8,4096]{2,1,0:T(8,128)(2,1)S(1)}, u32[]{:S(2)}, u32[]{:S(2)}) %collective-permute-start.8) | collective-permute-done | bytes 131104 | tf_op jit(solution)/shard_map/ppermute | solution.py:178
  32.4 2.0 %collective-permute-done.9 = bf16[2,8,4096]{2,1,0:T(8,128)(2,1)S(1)} collective-permute-done((bf16[2,8,4096]{2,1,0:T(8,128)(2,1)S(1)}, bf16[2,8,4096]{2,1,0:T(8,128)(2,1)S(1)}, u32[]{:S(2)}, u32[]{:S(2)}) %collective-permute-start.9) | collective-permute-done | bytes 131104 | tf_op jit(solution)/shard_map/ppermute | solution.py:178
  34.4 0.1 fusion.4
  34.5 0.1 fusion.5
  34.6 0.1 collective-permute-start.10
  34.7 3.5 %collective-permute-start.12 = (bf16[2,2,4096]{2,1,0:T(2,128)(2,1)S(1)}, bf16[2,2,4096]{2,1,0:T(2,128)(2,1)S(1)}, u32[]{:S(2)}, u32[]{:S(2)}) collective-permute-start(bf16[2,2,4096]{2,1,0:T(2,128)(2,1)S(1)} %get-tuple-element.33), channel_id=1, source_target_pairs={{0,24},{2,26},{4,28},{6,30},{8,16},{10,18},{12,20},{14,22},{16,8},... | collective-permute-start | bytes 98312 | tf_op jit(solution)/shard_map/ppermute | solution.py:178
  38.2 0.0 collective-permute-start.11
  38.2 3.2 %shard_map.110 = (bf16[48,128,128]{2,1,0:T(8,128)(2,1)}, bf16[48,128,128]{2,1,0:T(8,128)(2,1)}, bf16[48,128,128]{2,1,0:T(8,128)(2,1)}) custom-call(s32[3,2,48]{2,1,0:T(2,128)S(1)} %pad_add_fusion.idx, bf16[2,32,4096]{2,1,0:T(8,128)(2,1)S(1)} %pad_maximum_fusion.panel, bf16[3,4,32,128]{3,2,1,0:T(8,128)(2,1)S(1)} %get-tuple-element.23.acts), custom_call_target="tpu_custom_call" | custom-call | flops 150994944 | bytes 9437184 | tf_op jit(solution)/shard_map/pallas_call | solution.py:236
  41.3 0.0 collective-permute-done.10
  41.3 0.0 collective-permute-done.12
  41.4 1.6 %collective-permute-done.11 = bf16[2,2,4096]{2,1,0:T(2,128)(2,1)S(1)} collective-permute-done((bf16[2,2,4096]{2,1,0:T(2,128)(2,1)S(1)}, bf16[2,2,4096]{2,1,0:T(2,128)(2,1)S(1)}, u32[]{:S(2)}, u32[]{:S(2)}) %collective-permute-start.11) | collective-permute-done | bytes 32800 | tf_op jit(solution)/shard_map/ppermute | solution.py:178
  43.0 0.1 fusion.2
  43.0 0.6 %slice_bitcast_fusion = (bf16[2,4096]{1,0:T(2,128)(2,1)}, bf16[2,4096]{1,0:T(2,128)(2,1)}) fusion(bf16[2,2,4096]{2,1,0:T(2,128)(2,1)S(1)} %fusion.2), kind=kLoop, calls=%fused_computation.8 | loop fusion | bytes 65536 | tf_op jit(solution)/shard_map/squeeze | solution.py:264
  (5 shorter events, 0.1 us)
Async XLA Ops:
  1.4 7.0 %collective-permute-start.2 = (bf16[2,2,4096]{2,1,0:T(2,128)(2,1)S(1)}, bf16[2,2,4096]{2,1,0:T(2,128)(2,1)S(1)}, u32[]{:S(2)}, u32[]{:S(2)}) collective-permute-start(bf16[2,2,4096]{2,1,0:T(2,128)(2,1)S(1)} %pad_maximum_fusion.2), channel_id=1, source_target_pairs={{0,24},{2,26},{4,28},{6,30},{8,16},{10,18},{12,20},{14,22},{16,8},... | collective-permute-start | bytes 98312 | tf_op jit(solution)/shard_map/ppermute | solution.py:178
  6.6 4.8 %collective-permute-start.1 = (bf16[2,2,4096]{2,1,0:T(2,128)(2,1)S(1)}, bf16[2,2,4096]{2,1,0:T(2,128)(2,1)S(1)}, u32[]{:S(2)}, u32[]{:S(2)}) collective-permute-start(bf16[2,2,4096]{2,1,0:T(2,128)(2,1)S(1)} %pad_maximum_fusion.2), channel_id=1, source_target_pairs={{0,16},{2,18},{4,20},{6,22},{8,24},{10,26},{12,28},{14,30},{16,0},... | collective-permute-start | bytes 98312 | tf_op jit(solution)/shard_map/ppermute | solution.py:178
  6.6 4.8 %collective-permute-start = (bf16[2,2,4096]{2,1,0:T(2,128)(2,1)S(1)}, bf16[2,2,4096]{2,1,0:T(2,128)(2,1)S(1)}, u32[]{:S(2)}, u32[]{:S(2)}) collective-permute-start(bf16[2,2,4096]{2,1,0:T(2,128)(2,1)S(1)} %pad_maximum_fusion.2), channel_id=1, source_target_pairs={{0,8},{2,10},{4,12},{6,14},{8,0},{10,2},{12,4},{14,6},{16,24},{18,... | collective-permute-start | bytes 98312 | tf_op jit(solution)/shard_map/ppermute | solution.py:178
  11.5 7.3 %collective-permute-start.5 = (bf16[2,8,4096]{2,1,0:T(8,128)(2,1)S(1)}, bf16[2,8,4096]{2,1,0:T(8,128)(2,1)S(1)}, u32[]{:S(2)}, u32[]{:S(2)}) collective-permute-start(bf16[2,8,4096]{2,1,0:T(8,128)(2,1)S(1)} %pad_maximum_fusion.1), channel_id=1, source_target_pairs={{0,6},{2,4},{4,2},{6,0},{8,14},{10,12},{12,10},{14,8},{16,22},{18,... | collective-permute-start | bytes 393224 | tf_op jit(solution)/shard_map/ppermute | solution.py:178
  14.0 5.6 %collective-permute-start.4 = (bf16[2,8,4096]{2,1,0:T(8,128)(2,1)S(1)}, bf16[2,8,4096]{2,1,0:T(8,128)(2,1)S(1)}, u32[]{:S(2)}, u32[]{:S(2)}) collective-permute-start(bf16[2,8,4096]{2,1,0:T(8,128)(2,1)S(1)} %pad_maximum_fusion.1), channel_id=1, source_target_pairs={{0,4},{2,6},{4,0},{6,2},{8,12},{10,14},{12,8},{14,10},{16,20},{18,... | collective-permute-start | bytes 393224 | tf_op jit(solution)/shard_map/ppermute | solution.py:178
  14.6 5.1 %collective-permute-start.3 = (bf16[2,8,4096]{2,1,0:T(8,128)(2,1)S(1)}, bf16[2,8,4096]{2,1,0:T(8,128)(2,1)S(1)}, u32[]{:S(2)}, u32[]{:S(2)}) collective-permute-start(bf16[2,8,4096]{2,1,0:T(8,128)(2,1)S(1)} %pad_maximum_fusion.1), channel_id=1, source_target_pairs={{0,2},{2,0},{4,6},{6,4},{8,10},{10,8},{12,14},{14,12},{16,18},{18,... | collective-permute-start | bytes 393224 | tf_op jit(solution)/shard_map/ppermute | solution.py:178
  21.5 1.4 %collective-permute-start.6 = (f32[3,3,32,128]{3,2,1,0:T(8,128)S(1)}, f32[3,3,32,128]{3,2,1,0:T(8,128)S(1)}, u32[]{:S(2)}, u32[]{:S(2)}) collective-permute-start(f32[3,3,32,128]{3,2,1,0:T(8,128)S(1)} %forward.1.parts), channel_id=1, source_target_pairs={{0,1},{1,0},{2,3},{3,2},{4,5},{5,4},{6,7},{7,6},{8,9},{9,8},{10,11... | collective-permute-start | bytes 442376 | tf_op jit(solution)/shard_map/ppermute | solution.py:178
  25.2 6.4 %collective-permute-start.7 = (bf16[2,8,4096]{2,1,0:T(8,128)(2,1)S(1)}, bf16[2,8,4096]{2,1,0:T(8,128)(2,1)S(1)}, u32[]{:S(2)}, u32[]{:S(2)}) collective-permute-start(bf16[2,8,4096]{2,1,0:T(8,128)(2,1)S(1)} %get-tuple-element.20), channel_id=1, source_target_pairs={{0,2},{2,0},{4,6},{6,4},{8,10},{10,8},{12,14},{14,12},{16,18},{18,... | collective-permute-start | bytes 393224 | tf_op jit(solution)/shard_map/ppermute | solution.py:178
  26.3 6.1 %collective-permute-start.8 = (bf16[2,8,4096]{2,1,0:T(8,128)(2,1)S(1)}, bf16[2,8,4096]{2,1,0:T(8,128)(2,1)S(1)}, u32[]{:S(2)}, u32[]{:S(2)}) collective-permute-start(bf16[2,8,4096]{2,1,0:T(8,128)(2,1)S(1)} %get-tuple-element.21), channel_id=1, source_target_pairs={{0,4},{2,6},{4,0},{6,2},{8,12},{10,14},{12,8},{14,10},{16,20},{18,... | collective-permute-start | bytes 393224 | tf_op jit(solution)/shard_map/ppermute | solution.py:178
  27.1 7.3 %collective-permute-start.9 = (bf16[2,8,4096]{2,1,0:T(8,128)(2,1)S(1)}, bf16[2,8,4096]{2,1,0:T(8,128)(2,1)S(1)}, u32[]{:S(2)}, u32[]{:S(2)}) collective-permute-start(bf16[2,8,4096]{2,1,0:T(8,128)(2,1)S(1)} %get-tuple-element.22), channel_id=1, source_target_pairs={{0,6},{2,4},{4,2},{6,0},{8,14},{10,12},{12,10},{14,8},{16,22},{18,... | collective-permute-start | bytes 393224 | tf_op jit(solution)/shard_map/ppermute | solution.py:178
  34.6 6.8 %collective-permute-start.10 = (bf16[2,2,4096]{2,1,0:T(2,128)(2,1)S(1)}, bf16[2,2,4096]{2,1,0:T(2,128)(2,1)S(1)}, u32[]{:S(2)}, u32[]{:S(2)}) collective-permute-start(bf16[2,2,4096]{2,1,0:T(2,128)(2,1)S(1)} %get-tuple-element.32), channel_id=1, source_target_pairs={{0,8},{2,10},{4,12},{6,14},{8,0},{10,2},{12,4},{14,6},{16,24},{18,... | collective-permute-start | bytes 98312 | tf_op jit(solution)/shard_map/ppermute | solution.py:178
  34.7 6.7 %collective-permute-start.12 = (bf16[2,2,4096]{2,1,0:T(2,128)(2,1)S(1)}, bf16[2,2,4096]{2,1,0:T(2,128)(2,1)S(1)}, u32[]{:S(2)}, u32[]{:S(2)}) collective-permute-start(bf16[2,2,4096]{2,1,0:T(2,128)(2,1)S(1)} %get-tuple-element.33), channel_id=1, source_target_pairs={{0,24},{2,26},{4,28},{6,30},{8,16},{10,18},{12,20},{14,22},{16,8},... | collective-permute-start | bytes 98312 | tf_op jit(solution)/shard_map/ppermute | solution.py:178
  38.2 4.8 %collective-permute-start.11 = (bf16[2,2,4096]{2,1,0:T(2,128)(2,1)S(1)}, bf16[2,2,4096]{2,1,0:T(2,128)(2,1)S(1)}, u32[]{:S(2)}, u32[]{:S(2)}) collective-permute-start(bf16[2,2,4096]{2,1,0:T(2,128)(2,1)S(1)} %get-tuple-element.34), channel_id=1, source_target_pairs={{0,16},{2,18},{4,20},{6,22},{8,24},{10,26},{12,28},{14,30},{16,0},... | collective-permute-start | bytes 98312 | tf_op jit(solution)/shard_map/ppermute | solution.py:178

commit v2 on v1

--- a/solution.py
+++ b/solution.py
@@ -9,6 +9,7 @@
 
 
 HT = 3
+THIRD = 43691
 VM = pl.BlockSpec(memory_space=pltpu.VMEM)
 SM = pl.BlockSpec(memory_space=pltpu.SMEM)
 HBM = pl.BlockSpec(memory_space=pltpu.HBM)
@@ -28,9 +29,14 @@
     return pl.ds(pl.multiple_of(index * tile, tile), tile)
 
 
-def forward_kernel(group, idx, panel, gate, up, down, parts):
+def rows_of(panel_a, panel_b, which, block, tile):
+    where = lanes(block, tile)
+    return jnp.concatenate([panel_a[which, :, where], panel_b[which, :, where]], axis=0)
+
+
+def forward_kernel(group, idx, panel_a, panel_b, gate, up, down, parts):
     tile = gate.shape[-1]
-    rows = panel.shape[1]
+    rows = panel_a.shape[1] + panel_b.shape[1]
 
     def stacked(which, m, base):
         stack = []
@@ -38,7 +44,7 @@
             k = base + j
             block = idx[m, 0, k]
             col = idx[m, 1, k]
-            pick = panel[which, :, lanes(block, tile)]
+            pick = rows_of(panel_a, panel_b, which, block, tile)
             zero = jnp.zeros_like(pick)
             stack.append(
                 jnp.concatenate([jnp.where(col == c, pick, zero) for c in range(HT)], axis=0)
@@ -65,9 +71,9 @@
 
 
 def backward_kernel(
-    group, quarters, idx, parts, other, gate, up, down, acts, keep, *rest
+    group, quarters, idx, parts, other, gate, up, down, acts, *rest
 ):
-    sends, (out_sum, in_sum) = rest[:quarters - 1], rest[quarters - 1:]
+    keeps, sends, (out_sum, in_sum) = rest[:2], rest[2:-2], rest[-2:]
     tile = gate.shape[-1]
     rows = parts.shape[2]
     gate_sum = parts[0] + other[0]
@@ -109,14 +115,18 @@
             for j in range(group):
                 where = lanes(idx[m, 0, base + j], tile)
                 target[:, where] += products[j]
-    size = rows // quarters
-    for which, total in ((0, out_sum), (1, in_sum)):
-        keep[which] = total[:size]
-        for q in range(1, quarters):
-            sends[q - 1][which] = total[q * size:(q + 1) * size].astype(BF16)
-
-
-def grad_kernel(group, jobs, idx, panel, acts, *refs):
+    size = rows // (2 * quarters)
+    for h in range(2):
+        for q in range(quarters):
+            span = pl.ds((h * quarters + q) * size, size)
+            for which, total in ((0, out_sum), (1, in_sum)):
+                if q == 0:
+                    keeps[h][which] = total[span]
+                else:
+                    sends[h * (quarters - 1) + q - 1][which] = total[span].astype(BF16)
+
+
+def grad_kernel(group, jobs, idx, panel_a, panel_b, acts, *refs):
     outs, bufs, sem = refs[:len(jobs)], refs[len(jobs):-1], refs[-1]
     tile = outs[0].shape[-1]
     cap = outs[0].shape[0]
@@ -124,7 +134,7 @@
     for i, (m, which) in enumerate(jobs):
         for g in range(cap // group):
             for k in range(g * group, (g + 1) * group):
-                block = panel[which, :, lanes(idx[m, 0, k], tile)]
+                block = rows_of(panel_a, panel_b, which, idx[m, 0, k], tile)
                 act = acts[m, idx[m, 1, k]]
                 left, right = (act, block) if m == 2 else (block, act)
                 bufs[i][k] = lax.dot_general(
@@ -138,12 +148,33 @@
         copy.wait()
 
 
-def load_kernel(gate_in, up_in, down_in, gate, up, down, sem):
-    pairs = ((gate_in, gate), (up_in, up), (down_in, down))
+def load_kernel(
+    row_blocks, slots_in, counts_in, gate_in, up_in, down_in, gate, up, down, idx, slots, counts, sem
+):
+    pairs = (
+        (slots_in, slots),
+        (counts_in, counts),
+        (gate_in, gate),
+        (up_in, up),
+        (down_in, down),
+    )
     copies = [pltpu.make_async_copy(a, b, sem.at[i]) for i, (a, b) in enumerate(pairs)]
     for copy in copies:
         copy.start()
-    for copy in copies:
+    for copy in copies[:2]:
+        copy.wait()
+    for m in range(3):
+        spot = slots[m]
+        if m == 2:
+            column = sum((spot >= c * row_blocks).astype(jnp.int32) for c in range(1, HT))
+            block = spot - column * row_blocks
+        else:
+            block = lax.shift_right_logical(spot * THIRD, 17)
+            column = spot - block * HT
+        order = lax.broadcasted_iota(jnp.int32, spot.shape, 1)
+        idx[m, 0:1] = block
+        idx[m, 1:2] = jnp.where(order < counts[m], column, HT)
+    for copy in copies[2:]:
         copy.wait()
 
 
@@ -177,66 +208,66 @@
         size = lax.axis_size(axis)
         return lax.ppermute(x, axis, [(i, i ^ bit) for i in range(size)])
 
-    slots = kept_slots[:, 0, 0]
-    counts = kept_counts[:, 0, 0]
-    live = jnp.arange(cap, dtype=jnp.int32)[None] < counts[:, None]
-    is_down = jnp.arange(3)[:, None] == 2
-    minor = jnp.where(is_down, row_blocks, HT)
-    major_pos, minor_pos = slots // minor, slots % minor
-    block = jnp.where(is_down, minor_pos, major_pos)
-    column = jnp.where(live, jnp.where(is_down, major_pos, minor_pos), HT)
-    idx = jnp.stack([block, column], axis=1)
-
-    gate, up, down = pl.pallas_call(
-        load_kernel,
-        out_shape=[pltpu.VMEM((cap, tile, tile), BF16)] * 3,
-        in_specs=[HBM] * 3,
-        out_specs=[VM] * 3,
-        scratch_shapes=[pltpu.SemaphoreType.DMA((3,))],
-        compiler_params=pltpu.CompilerParams(vmem_limit_bytes=58 << 20),
+    gate, up, down, idx = pl.pallas_call(
+        functools.partial(load_kernel, row_blocks),
+        out_shape=[pltpu.VMEM((cap, tile, tile), BF16)] * 3
+        + [pltpu.VMEM((3, 2, cap), jnp.int32)],
+        in_specs=[HBM] * 5,
+        out_specs=[VM] * 4,
+        scratch_shapes=[
+            pltpu.VMEM((3, 1, cap), jnp.int32),
+            pltpu.SMEM((3,), jnp.int32),
+            pltpu.SemaphoreType.DMA((5,)),
+        ],
+        compiler_params=pltpu.CompilerParams(vmem_limit_bytes=57 << 20),
         name="load",
-    )(gate_tiles[0, 0], up_tiles[0, 0], down_tiles[0, 0])
+    )(kept_slots[:, 0], kept_counts[:, 0, 0], gate_tiles[0, 0], up_tiles[0, 0], down_tiles[0, 0])
 
     held = lax.optimization_barrier(jnp.stack([tokens, cotangent]))
-    for stage in stages[::-1]:
+    for stage in stages[:1:-1]:
         pieces = [held] + [swap(held, offset) for offset in stage[1:]]
         held = lax.optimization_barrier(jnp.concatenate(pieces, axis=1))
-    panel = held
+    pieces = [held] + [swap(held, offset) for offset in stages[1][1:]]
+    half = len(pieces) // 2
+    halves = []
+    for part in (pieces[:half], pieces[half:]):
+        halves.append(lax.optimization_barrier(jnp.concatenate(part, axis=1)))
+    quarter_rows = [[part] + [swap(part, offset) for offset in stages[0][1:]] for part in halves]
+    panels = [lax.optimization_barrier(jnp.concatenate(part, axis=1)) for part in quarter_rows]
 
     parts = pl.pallas_call(
         functools.partial(forward_kernel, group),
         out_shape=pltpu.VMEM((3, HT, rows, tile), F32),
-        in_specs=[SM, VM, VM, VM, VM],
+        in_specs=[SM] + [VM] * 5,
         out_specs=VM,
         compiler_params=VLIM,
         name="forward",
-    )(idx, panel, gate, up, down)
+    )(idx, *panels, gate, up, down)
 
     narrow_bits = bits_of(n_narrow)
     for bit in narrow_bits[:-1]:
         parts = parts + swap(parts, bit, "narrow")
     other = swap(parts, narrow_bits[-1], "narrow")
 
-    size = rows // quarters
-    acts, keep, *sends = pl.pallas_call(
+    size = rows // (2 * quarters)
+    acts, *moved = pl.pallas_call(
         functools.partial(backward_kernel, group, quarters),
-        out_shape=[
-            jax.ShapeDtypeStruct((3, HT + 1, rows, tile), BF16),
-            jax.ShapeDtypeStruct((2, size, feats), F32),
-        ]
-        + [jax.ShapeDtypeStruct((2, size, feats), BF16)] * (quarters - 1),
+        out_shape=[jax.ShapeDtypeStruct((3, HT + 1, rows, tile), BF16)]
+        + [jax.ShapeDtypeStruct((2, size, feats), F32)] * 2
+        + [jax.ShapeDtypeStruct((2, size, feats), BF16)] * (2 * quarters - 2),
         in_specs=[SM] + [VM] * 5,
-        out_specs=[VM] * (quarters + 1),
+        out_specs=[VM] * (2 * quarters + 1),
         scratch_shapes=[pltpu.VMEM((rows, feats), F32)] * 2,
         compiler_params=VLIM,
         name="backward",
     )(idx, parts, other, gate, up, down)
+    keeps, sends = moved[:2], [moved[2:quarters + 1], moved[quarters + 1:]]
 
     def tile_grads(jobs):
         return pl.pallas_call(
             functools.partial(grad_kernel, group, jobs),
             out_shape=[jax.ShapeDtypeStruct((cap, tile, tile), BF16)] * len(jobs),
-            in_specs=[SM, VM, VM],
+            in_specs=[SM, VM, VM, VM],
             out_specs=[HBM] * len(jobs),
             scratch_shapes=[pltpu.VMEM((cap, tile, tile), BF16)] * len(jobs)
             + [pltpu.SemaphoreType.DMA((len(jobs), cap // group))],
@@ -246,13 +277,24 @@
                 transcendentals=0,
             ),
             compiler_params=VLIM,
-        )(idx, panel, acts)
-
-    got = [swap(s, offset) for s, offset in zip(sends, stages[0][1:])]
-    total = keep
-    for g in got:
-        total = total + g.astype(F32)
-    for stage in stages[1:]:
+        )(idx, *panels, acts)
+
+    got = {h: [swap(s, offset) for s, offset in zip(sends[h], stages[0][1:])] for h in (1, 0)}
+    blocks = {}
+    for h in (1, 0):
+        total = keeps[h]
+        for g in got[h]:
+            total = total + g.astype(F32)
+        count = len(stages[1]) // 2
+        step = size // count
+        for i in range(count):
+            blocks[h * count + i] = total[:, i * step:(i + 1) * step]
+            if h * count + i:
+                blocks[h * count + i] = blocks[h * count + i].astype(BF16)
+    total = blocks[0]
+    for i, offset in enumerate(stages[1][1:], 1):
+        total = total + swap(blocks[i], offset).astype(F32)
+    for stage in stages[2:]:
         size = total.shape[1] // len(stage)
         pieces = [total[:, q * size:(q + 1) * size] for q in range(len(stage))]
         total = pieces[0]

time: 44 us -> 46.7 us (1.061)
  starting transfers between devices: 16.5 us -> 26.3 us
  waiting for transfers between devices: 13.2 us -> 7.62 us
  other arithmetic: 2.87 us -> 1.4 us
    ppermute x13 -> x19, starting transfers between devices: 16.5 us -> 26.3 us  [swap(): return lax.ppermute(x, axis, [(i, i ^ bit) for i in range(size)])]
    ppermute x13 -> x19, waiting for transfers between devices: 13.2 us -> 7.62 us  [swap(): return lax.ppermute(x, axis, [(i, i ^ bit) for i in range(size)])]
    select_n x3 -> x0, other arithmetic: 1.75 us -> none  [the longest x1 1.02 us: per_device(): block = jnp.where(is_down, minor_pos, major_pos)]
  transfers between devices with their start and end apart: 13 -> 19, of which waited for: 9 -> 8; matrix products, arithmetic and copies ran while one was open for 4% -> 1% of each run, Pallas kernels for 13% -> 12%
where the time goes in v2:
time: 46.7 us; the launch traced here: 46.4 us
  starting transfers between devices  26.3 us (56%)
  Pallas kernels  9.59 us (21%)
  waiting for transfers between devices  7.62 us (16%)
  other arithmetic  1.4 us (3%)
  between operations  0.76 us (2%)
  local copies, waits for them, and re-layouts  0.72 us (2%)
    ppermute x19, starting transfers between devices, swap(): return lax.ppermute(x, axis, [(i, i ^ bit) for i in range(size)])  26.3 us
    ppermute x19, waiting for transfers between devices, swap(): return lax.ppermute(x, axis, [(i, i ^ bit) for i in range(size)])  7.62 us
    pallas_call x1, Pallas kernels, tile_grads(): pl.pallas_call(functools.partial(grad_kernel, group, jobs), out_shape=[ja...  3.17 us
    pallas_call x1, Pallas kernels, per_device(): pl.pallas_call(functools.partial(load_kernel, row_blocks), out_shape=[plt...  2.41 us
    pallas_call x1, Pallas kernels, per_device(): pl.pallas_call(functools.partial(backward_kernel, group, quarters), out_s...  2.21 us
    pallas_call x1, Pallas kernels, per_device(): pl.pallas_call(functools.partial(forward_kernel, group), out_shape=pltpu....  1.8 us
  transfers between devices with their start and end apart: 19, of which 8 were waited for; matrix products, arithmetic and copies ran while one was open for 1% of the time, Pallas kernels for 12%

profile of v2, /device:TPU:0, one launch (start us, length us, event | category | flops | bytes accessed | tf_op | source)
XLA Modules:
  0.0 46.4 jit_solution(7011078728626014670)
XLA Ops:
  0.6 0.8 %pad_maximum_fusion.4 = bf16[2,2,4096]{2,1,0:T(2,128)(2,1)S(1)} fusion(bf16[1,2,4096]{2,1,0:T(2,128)(2,1)} %bitcast.28, bf16[1,2,4096]{2,1,0:T(2,128)(2,1)} %bitcast.29), kind=kLoop, calls=%fused_computation.11 | loop fusion | flops 16384 | bytes 65536 | tf_op jit(solution)/shard_map/stack | solution.py:226
  1.4 3.1 %collective-permute-start = (bf16[2,2,4096]{2,1,0:T(2,128)(2,1)S(1)}, bf16[2,2,4096]{2,1,0:T(2,128)(2,1)S(1)}, u32[]{:S(2)}, u32[]{:S(2)}) collective-permute-start(bf16[2,2,4096]{2,1,0:T(2,128)(2,1)S(1)} %pad_maximum_fusion.4), channel_id=1, source_target_pairs={{0,8},{2,10},{4,12},{6,14},{8,0},{10,2},{12,4},{14,6},{16,24},{18,... | collective-permute-start | bytes 98312 | tf_op jit(solution)/shard_map/ppermute | solution.py:209
  4.5 2.5 %collective-permute-start.5 = (bf16[2,2,4096]{2,1,0:T(2,128)(2,1)S(1)}, bf16[2,2,4096]{2,1,0:T(2,128)(2,1)S(1)}, u32[]{:S(2)}, u32[]{:S(2)}) collective-permute-start(bf16[2,2,4096]{2,1,0:T(2,128)(2,1)S(1)} %pad_maximum_fusion.4), channel_id=1, source_target_pairs={{0,24},{2,26},{4,28},{6,30},{8,16},{10,18},{12,20},{14,22},{16,8},... | collective-permute-start | bytes 98312 | tf_op jit(solution)/shard_map/ppermute | solution.py:209
  7.0 0.1 collective-permute-start.4
  7.1 2.4 %load.1 = (bf16[48,128,128]{2,1,0:T(8,128)(2,1)S(1)}, bf16[48,128,128]{2,1,0:T(8,128)(2,1)S(1)}, bf16[48,128,128]{2,1,0:T(8,128)(2,1)S(1)}, s32[3,2,48]{2,1,0:T(2,128)S(1)}) custom-call(s32[3,1,48]{2,1,0:T(1,128)} %bitcast.30, s32[3]{0:T(128)} %bitcast.31, bf16[48,128,128]{2,1,0:T(8,128)(2,1)} %bitcast.20, bf16[48,128,128]{2,1,0:T(8,128)(2,1)} %bitcast.21, ...), custom_call_target="tpu_custom_call" | custom-call | tf_op jit(solution)/shard_map/load/pallas_call | solution.py:211
  9.5 0.0 collective-permute-done
  9.6 0.1 pad_maximum_fusion.2
  9.6 2.5 %collective-permute-start.3 = (bf16[2,4,4096]{2,1,0:T(4,128)(2,1)S(1)}, bf16[2,4,4096]{2,1,0:T(4,128)(2,1)S(1)}, u32[]{:S(2)}, u32[]{:S(2)}) collective-permute-start(bf16[2,4,4096]{2,1,0:T(4,128)(2,1)S(1)} %pad_maximum_fusion.2), channel_id=1, source_target_pairs={{0,6},{2,4},{4,2},{6,0},{8,14},{10,12},{12,10},{14,8},{16,22},{18,... | collective-permute-start | bytes 196616 | tf_op jit(solution)/shard_map/ppermute | solution.py:209
  12.2 0.5 %collective-permute-start.2 = (bf16[2,4,4096]{2,1,0:T(4,128)(2,1)S(1)}, bf16[2,4,4096]{2,1,0:T(4,128)(2,1)S(1)}, u32[]{:S(2)}, u32[]{:S(2)}) collective-permute-start(bf16[2,4,4096]{2,1,0:T(4,128)(2,1)S(1)} %pad_maximum_fusion.2), channel_id=1, source_target_pairs={{0,4},{2,6},{4,0},{6,2},{8,12},{10,14},{12,8},{14,10},{16,20},{18,... | collective-permute-start | bytes 196616 | tf_op jit(solution)/shard_map/ppermute | solution.py:209
  12.7 0.5 %collective-permute-start.1 = (bf16[2,4,4096]{2,1,0:T(4,128)(2,1)S(1)}, bf16[2,4,4096]{2,1,0:T(4,128)(2,1)S(1)}, u32[]{:S(2)}, u32[]{:S(2)}) collective-permute-start(bf16[2,4,4096]{2,1,0:T(4,128)(2,1)S(1)} %pad_maximum_fusion.2), channel_id=1, source_target_pairs={{0,2},{2,0},{4,6},{6,4},{8,10},{10,8},{12,14},{14,12},{16,18},{18,... | collective-permute-start | bytes 196616 | tf_op jit(solution)/shard_map/ppermute | solution.py:209
  13.2 0.0 collective-permute-done.5
  13.2 0.0 collective-permute-done.4
  13.2 0.1 pad_maximum_fusion.3
  13.3 2.5 %collective-permute-start.8 = (bf16[2,4,4096]{2,1,0:T(4,128)(2,1)S(1)}, bf16[2,4,4096]{2,1,0:T(4,128)(2,1)S(1)}, u32[]{:S(2)}, u32[]{:S(2)}) collective-permute-start(bf16[2,4,4096]{2,1,0:T(4,128)(2,1)S(1)} %pad_maximum_fusion.3), channel_id=1, source_target_pairs={{0,6},{2,4},{4,2},{6,0},{8,14},{10,12},{12,10},{14,8},{16,22},{18,... | collective-permute-start | bytes 196616 | tf_op jit(solution)/shard_map/ppermute | solution.py:209
  15.8 0.5 %collective-permute-start.7 = (bf16[2,4,4096]{2,1,0:T(4,128)(2,1)S(1)}, bf16[2,4,4096]{2,1,0:T(4,128)(2,1)S(1)}, u32[]{:S(2)}, u32[]{:S(2)}) collective-permute-start(bf16[2,4,4096]{2,1,0:T(4,128)(2,1)S(1)} %pad_maximum_fusion.3), channel_id=1, source_target_pairs={{0,4},{2,6},{4,0},{6,2},{8,12},{10,14},{12,8},{14,10},{16,20},{18,... | collective-permute-start | bytes 196616 | tf_op jit(solution)/shard_map/ppermute | solution.py:209
  16.3 0.0 collective-permute-done.3
  16.3 0.8 %collective-permute-start.6 = (bf16[2,4,4096]{2,1,0:T(4,128)(2,1)S(1)}, bf16[2,4,4096]{2,1,0:T(4,128)(2,1)S(1)}, u32[]{:S(2)}, u32[]{:S(2)}) collective-permute-start(bf16[2,4,4096]{2,1,0:T(4,128)(2,1)S(1)} %pad_maximum_fusion.3), channel_id=1, source_target_pairs={{0,2},{2,0},{4,6},{6,4},{8,10},{10,8},{12,14},{14,12},{16,18},{18,... | collective-permute-start | bytes 196616 | tf_op jit(solution)/shard_map/ppermute | solution.py:209
  17.1 0.5 collective-permute-done.2
  17.5 0.0 collective-permute-done.1
  17.5 0.2 pad_maximum_fusion.panel_a
  17.7 1.6 %collective-permute-done.8 = bf16[2,4,4096]{2,1,0:T(4,128)(2,1)S(1)} collective-permute-done((bf16[2,4,4096]{2,1,0:T(4,128)(2,1)S(1)}, bf16[2,4,4096]{2,1,0:T(4,128)(2,1)S(1)}, u32[]{:S(2)}, u32[]{:S(2)}) %collective-permute-start.8) | collective-permute-done | bytes 65568 | tf_op jit(solution)/shard_map/ppermute | solution.py:209
  19.3 0.8 %collective-permute-done.7 = bf16[2,4,4096]{2,1,0:T(4,128)(2,1)S(1)} collective-permute-done((bf16[2,4,4096]{2,1,0:T(4,128)(2,1)S(1)}, bf16[2,4,4096]{2,1,0:T(4,128)(2,1)S(1)}, u32[]{:S(2)}, u32[]{:S(2)}) %collective-permute-start.7) | collective-permute-done | bytes 65568 | tf_op jit(solution)/shard_map/ppermute | solution.py:209
  20.1 0.5 %collective-permute-done.6 = bf16[2,4,4096]{2,1,0:T(4,128)(2,1)S(1)} collective-permute-done((bf16[2,4,4096]{2,1,0:T(4,128)(2,1)S(1)}, bf16[2,4,4096]{2,1,0:T(4,128)(2,1)S(1)}, u32[]{:S(2)}, u32[]{:S(2)}) %collective-permute-start.6) | collective-permute-done | bytes 65568 | tf_op jit(solution)/shard_map/ppermute | solution.py:209
  20.6 0.2 pad_maximum_fusion.1.panel_b
  20.7 1.8 %forward.1.parts = f32[3,3,32,128]{3,2,1,0:T(8,128)S(1)} custom-call(s32[3,2,48]{2,1,0:T(2,128)S(1)} %get-tuple-element.21.idx, bf16[2,16,4096]{2,1,0:T(8,128)(2,1)S(1)} %pad_maximum_fusion.panel_a, bf16[2,16,4096]{2,1,0:T(8,128)(2,1)S(1)} %pad_maximum_fusion.1.panel_b, bf16[48,128,128]{2,1,0:T(8,128)(2,1)S(1)} %get-tuple-element.22.gate, ...), custom_call_target="tpu_custom_call" | custom-call | tf_op jit(solution)/shard_map/forward/pallas_call | solution.py:238
  22.5 0.1 collective-permute-start.9
  22.6 1.4 %collective-permute-done.9.other = f32[3,3,32,128]{3,2,1,0:T(8,128)S(1)} collective-permute-done((f32[3,3,32,128]{3,2,1,0:T(8,128)S(1)}, f32[3,3,32,128]{3,2,1,0:T(8,128)S(1)}, u32[]{:S(2)}, u32[]{:S(2)}) %collective-permute-start.9) | collective-permute-done | bytes 147488 | tf_op jit(solution)/shard_map/ppermute | solution.py:209
  24.0 2.2 %backward.1 = (bf16[3,4,32,128]{3,2,1,0:T(8,128)(2,1)S(1)}, f32[2,4,4096]{2,1,0:T(4,128)S(1)}, f32[2,4,4096]{2,1,0:T(4,128)S(1)}, bf16[2,4,4096]{2,1,0:T(4,128)(...) custom-call(s32[3,2,48]{2,1,0:T(2,128)S(1)} %get-tuple-element.21.id, ...), custom_call_target="tpu_custom_call" | custom-call | tf_op jit(solution)/shard_map/backward/pallas_call | solution.py:253
  26.2 0.8 %collective-permute-start.10 = (bf16[2,4,4096]{2,1,0:T(4,128)(2,1)S(1)}, bf16[2,4,4096]{2,1,0:T(4,128)(2,1)S(1)}, u32[]{:S(2)}, u32[]{:S(2)}) collective-permute-start(bf16[2,4,4096]{2,1,0:T(4,128)(2,1)S(1)} %get-tuple-element.26), channel_id=1, source_target_pairs={{0,2},{2,0},{4,6},{6,4},{8,10},{10,8},{12,14},{14,12},{16,18},{18,... | collective-permute-start | bytes 196616 | tf_op jit(solution)/shard_map/ppermute | solution.py:209
  27.0 1.3 %collective-permute-start.11 = (bf16[2,4,4096]{2,1,0:T(4,128)(2,1)S(1)}, bf16[2,4,4096]{2,1,0:T(4,128)(2,1)S(1)}, u32[]{:S(2)}, u32[]{:S(2)}) collective-permute-start(bf16[2,4,4096]{2,1,0:T(4,128)(2,1)S(1)} %get-tuple-element.27), channel_id=1, source_target_pairs={{0,4},{2,6},{4,0},{6,2},{8,12},{10,14},{12,8},{14,10},{16,20},{18,... | collective-permute-start | bytes 196616 | tf_op jit(solution)/shard_map/ppermute | solution.py:209
  28.3 1.4 %collective-permute-start.12 = (bf16[2,4,4096]{2,1,0:T(4,128)(2,1)S(1)}, bf16[2,4,4096]{2,1,0:T(4,128)(2,1)S(1)}, u32[]{:S(2)}, u32[]{:S(2)}) collective-permute-start(bf16[2,4,4096]{2,1,0:T(4,128)(2,1)S(1)} %get-tuple-element.28), channel_id=1, source_target_pairs={{0,6},{2,4},{4,2},{6,0},{8,14},{10,12},{12,10},{14,8},{16,22},{18,... | collective-permute-start | bytes 196616 | tf_op jit(solution)/shard_map/ppermute | solution.py:209
  29.7 0.8 %collective-permute-start.14 = (bf16[2,4,4096]{2,1,0:T(4,128)(2,1)S(1)}, bf16[2,4,4096]{2,1,0:T(4,128)(2,1)S(1)}, u32[]{:S(2)}, u32[]{:S(2)}) collective-permute-start(bf16[2,4,4096]{2,1,0:T(4,128)(2,1)S(1)} %get-tuple-element.30), channel_id=1, source_target_pairs={{0,2},{2,0},{4,6},{6,4},{8,10},{10,8},{12,14},{14,12},{16,18},{18,... | collective-permute-start | bytes 196616 | tf_op jit(solution)/shard_map/ppermute | solution.py:209
  30.5 1.3 %collective-permute-start.15 = (bf16[2,4,4096]{2,1,0:T(4,128)(2,1)S(1)}, bf16[2,4,4096]{2,1,0:T(4,128)(2,1)S(1)}, u32[]{:S(2)}, u32[]{:S(2)}) collective-permute-start(bf16[2,4,4096]{2,1,0:T(4,128)(2,1)S(1)} %get-tuple-element.31), channel_id=1, source_target_pairs={{0,4},{2,6},{4,0},{6,2},{8,12},{10,14},{12,8},{14,10},{16,20},{18,... | collective-permute-start | bytes 196616 | tf_op jit(solution)/shard_map/ppermute | solution.py:209
  31.8 1.4 %collective-permute-start.16 = (bf16[2,4,4096]{2,1,0:T(4,128)(2,1)S(1)}, bf16[2,4,4096]{2,1,0:T(4,128)(2,1)S(1)}, u32[]{:S(2)}, u32[]{:S(2)}) collective-permute-start(bf16[2,4,4096]{2,1,0:T(4,128)(2,1)S(1)} %get-tuple-element.32), channel_id=1, source_target_pairs={{0,6},{2,4},{4,2},{6,0},{8,14},{10,12},{12,10},{14,8},{16,22},{18,... | collective-permute-start | bytes 196616 | tf_op jit(solution)/shard_map/ppermute | solution.py:209
  33.2 0.0 collective-permute-done.11
  33.2 0.8 %collective-permute-done.12 = bf16[2,4,4096]{2,1,0:T(4,128)(2,1)S(1)} collective-permute-done((bf16[2,4,4096]{2,1,0:T(4,128)(2,1)S(1)}, bf16[2,4,4096]{2,1,0:T(4,128)(2,1)S(1)}, u32[]{:S(2)}, u32[]{:S(2)}) %collective-permute-start.12) | collective-permute-done | bytes 65568 | tf_op jit(solution)/shard_map/ppermute | solution.py:209
  34.1 1.9 %collective-permute-start.13 = (bf16[2,2,4096]{2,1,0:T(2,128)(2,1)S(1)}, bf16[2,2,4096]{2,1,0:T(2,128)(2,1)S(1)}, u32[]{:S(2)}, u32[]{:S(2)}) collective-permute-start(bf16[2,2,4096]{2,1,0:T(2,128)(2,1)S(1)} %slice.43), channel_id=1, source_target_pairs={{0,8},{2,10},{4,12},{6,14},{8,0},{10,2},{12,4},{14,6},{16,24},{18,... | collective-permute-start | bytes 98312 | tf_op jit(solution)/shard_map/ppermute | solution.py:209
  36.0 0.0 collective-permute-done.14
  36.0 0.0 collective-permute-done.15
  36.0 1.0 %collective-permute-done.16 = bf16[2,4,4096]{2,1,0:T(4,128)(2,1)S(1)} collective-permute-done((bf16[2,4,4096]{2,1,0:T(4,128)(2,1)S(1)}, bf16[2,4,4096]{2,1,0:T(4,128)(2,1)S(1)}, u32[]{:S(2)}, u32[]{:S(2)}) %collective-permute-start.16) | collective-permute-done | bytes 65568 | tf_op jit(solution)/shard_map/ppermute | solution.py:209
  37.0 0.1 add_convert_fusion
  37.1 2.9 %collective-permute-start.17 = (bf16[2,2,4096]{2,1,0:T(2,128)(2,1)S(1)}, bf16[2,2,4096]{2,1,0:T(2,128)(2,1)S(1)}, u32[]{:S(2)}, u32[]{:S(2)}) collective-permute-start(bf16[2,2,4096]{2,1,0:T(2,128)(2,1)S(1)} %get-tuple-element.37), channel_id=1, source_target_pairs={{0,16},{2,18},{4,20},{6,22},{8,24},{10,26},{12,28},{14,30},{16,0},... | collective-permute-start | bytes 98312 | tf_op jit(solution)/shard_map/ppermute | solution.py:209
  40.0 1.4 %collective-permute-start.18 = (bf16[2,2,4096]{2,1,0:T(2,128)(2,1)S(1)}, bf16[2,2,4096]{2,1,0:T(2,128)(2,1)S(1)}, u32[]{:S(2)}, u32[]{:S(2)}) collective-permute-start(bf16[2,2,4096]{2,1,0:T(2,128)(2,1)S(1)} %get-tuple-element.38), channel_id=1, source_target_pairs={{0,24},{2,26},{4,28},{6,30},{8,16},{10,18},{12,20},{14,22},{16,8},... | collective-permute-start | bytes 98312 | tf_op jit(solution)/shard_map/ppermute | solution.py:209
  41.3 3.2 %shard_map.110 = (bf16[48,128,128]{2,1,0:T(8,128)(2,1)}, bf16[48,128,128]{2,1,0:T(8,128)(2,1)}, bf16[48,128,128]{2,1,0:T(8,128)(2,1)}) custom-call(s32[3,2,48]{2,1,0:T(2,128)S(1)} %get-tuple-element.21.idx, bf16[2,16,4096]{2,1,0:T(8,128)(2,1)S(1)} %pad_maximum_fusion.panel_a, bf16[2,16,4096]{2,1,0:T(8,128)(2,1)S(1)} %pad_maximum_fusion.1.panel_b, ...), custom_call_target="tpu_custom_call" | custom-call | flops 150994944 | bytes 9437184 | tf_op jit(solution)/shard_map/pallas_call | solution.py:267
  44.5 0.0 collective-permute-done.13
  44.5 1.1 %collective-permute-done.18 = bf16[2,2,4096]{2,1,0:T(2,128)(2,1)S(1)} collective-permute-done((bf16[2,2,4096]{2,1,0:T(2,128)(2,1)S(1)}, bf16[2,2,4096]{2,1,0:T(2,128)(2,1)S(1)}, u32[]{:S(2)}, u32[]{:S(2)}) %collective-permute-start.18) | collective-permute-done | bytes 32800 | tf_op jit(solution)/shard_map/ppermute | solution.py:209
  45.7 0.1 fusion.2
  45.7 0.6 %slice_bitcast_fusion = (bf16[2,4096]{1,0:T(2,128)(2,1)}, bf16[2,4096]{1,0:T(2,128)(2,1)}) fusion(bf16[2,2,4096]{2,1,0:T(2,128)(2,1)S(1)} %fusion.2), kind=kLoop, calls=%fused_computation.12 | loop fusion | bytes 65536 | tf_op jit(solution)/shard_map/squeeze | solution.py:306
  (5 shorter events, 0.1 us)
Async XLA Ops:
  1.4 8.1 %collective-permute-start = (bf16[2,2,4096]{2,1,0:T(2,128)(2,1)S(1)}, bf16[2,2,4096]{2,1,0:T(2,128)(2,1)S(1)}, u32[]{:S(2)}, u32[]{:S(2)}) collective-permute-start(bf16[2,2,4096]{2,1,0:T(2,128)(2,1)S(1)} %pad_maximum_fusion.4), channel_id=1, source_target_pairs={{0,8},{2,10},{4,12},{6,14},{8,0},{10,2},{12,4},{14,6},{16,24},{18,... | collective-permute-start | bytes 98312 | tf_op jit(solution)/shard_map/ppermute | solution.py:209
  4.5 8.7 %collective-permute-start.5 = (bf16[2,2,4096]{2,1,0:T(2,128)(2,1)S(1)}, bf16[2,2,4096]{2,1,0:T(2,128)(2,1)S(1)}, u32[]{:S(2)}, u32[]{:S(2)}) collective-permute-start(bf16[2,2,4096]{2,1,0:T(2,128)(2,1)S(1)} %pad_maximum_fusion.4), channel_id=1, source_target_pairs={{0,24},{2,26},{4,28},{6,30},{8,16},{10,18},{12,20},{14,22},{16,8},... | collective-permute-start | bytes 98312 | tf_op jit(solution)/shard_map/ppermute | solution.py:209
  7.0 6.2 %collective-permute-start.4 = (bf16[2,2,4096]{2,1,0:T(2,128)(2,1)S(1)}, bf16[2,2,4096]{2,1,0:T(2,128)(2,1)S(1)}, u32[]{:S(2)}, u32[]{:S(2)}) collective-permute-start(bf16[2,2,4096]{2,1,0:T(2,128)(2,1)S(1)} %pad_maximum_fusion.4), channel_id=1, source_target_pairs={{0,16},{2,18},{4,20},{6,22},{8,24},{10,26},{12,28},{14,30},{16,0},... | collective-permute-start | bytes 98312 | tf_op jit(solution)/shard_map/ppermute | solution.py:209
  9.6 6.7 %collective-permute-start.3 = (bf16[2,4,4096]{2,1,0:T(4,128)(2,1)S(1)}, bf16[2,4,4096]{2,1,0:T(4,128)(2,1)S(1)}, u32[]{:S(2)}, u32[]{:S(2)}) collective-permute-start(bf16[2,4,4096]{2,1,0:T(4,128)(2,1)S(1)} %pad_maximum_fusion.2), channel_id=1, source_target_pairs={{0,6},{2,4},{4,2},{6,0},{8,14},{10,12},{12,10},{14,8},{16,22},{18,... | collective-permute-start | bytes 196616 | tf_op jit(solution)/shard_map/ppermute | solution.py:209
  12.2 5.4 %collective-permute-start.2 = (bf16[2,4,4096]{2,1,0:T(4,128)(2,1)S(1)}, bf16[2,4,4096]{2,1,0:T(4,128)(2,1)S(1)}, u32[]{:S(2)}, u32[]{:S(2)}) collective-permute-start(bf16[2,4,4096]{2,1,0:T(4,128)(2,1)S(1)} %pad_maximum_fusion.2), channel_id=1, source_target_pairs={{0,4},{2,6},{4,0},{6,2},{8,12},{10,14},{12,8},{14,10},{16,20},{18,... | collective-permute-start | bytes 196616 | tf_op jit(solution)/shard_map/ppermute | solution.py:209
  12.7 4.9 %collective-permute-start.1 = (bf16[2,4,4096]{2,1,0:T(4,128)(2,1)S(1)}, bf16[2,4,4096]{2,1,0:T(4,128)(2,1)S(1)}, u32[]{:S(2)}, u32[]{:S(2)}) collective-permute-start(bf16[2,4,4096]{2,1,0:T(4,128)(2,1)S(1)} %pad_maximum_fusion.2), channel_id=1, source_target_pairs={{0,2},{2,0},{4,6},{6,4},{8,10},{10,8},{12,14},{14,12},{16,18},{18,... | collective-permute-start | bytes 196616 | tf_op jit(solution)/shard_map/ppermute | solution.py:209
  13.3 6.0 %collective-permute-start.8 = (bf16[2,4,4096]{2,1,0:T(4,128)(2,1)S(1)}, bf16[2,4,4096]{2,1,0:T(4,128)(2,1)S(1)}, u32[]{:S(2)}, u32[]{:S(2)}) collective-permute-start(bf16[2,4,4096]{2,1,0:T(4,128)(2,1)S(1)} %pad_maximum_fusion.3), channel_id=1, source_target_pairs={{0,6},{2,4},{4,2},{6,0},{8,14},{10,12},{12,10},{14,8},{16,22},{18,... | collective-permute-start | bytes 196616 | tf_op jit(solution)/shard_map/ppermute | solution.py:209
  15.8 4.3 %collective-permute-start.7 = (bf16[2,4,4096]{2,1,0:T(4,128)(2,1)S(1)}, bf16[2,4,4096]{2,1,0:T(4,128)(2,1)S(1)}, u32[]{:S(2)}, u32[]{:S(2)}) collective-permute-start(bf16[2,4,4096]{2,1,0:T(4,128)(2,1)S(1)} %pad_maximum_fusion.3), channel_id=1, source_target_pairs={{0,4},{2,6},{4,0},{6,2},{8,12},{10,14},{12,8},{14,10},{16,20},{18,... | collective-permute-start | bytes 196616 | tf_op jit(solution)/shard_map/ppermute | solution.py:209
  16.3 4.3 %collective-permute-start.6 = (bf16[2,4,4096]{2,1,0:T(4,128)(2,1)S(1)}, bf16[2,4,4096]{2,1,0:T(4,128)(2,1)S(1)}, u32[]{:S(2)}, u32[]{:S(2)}) collective-permute-start(bf16[2,4,4096]{2,1,0:T(4,128)(2,1)S(1)} %pad_maximum_fusion.3), channel_id=1, source_target_pairs={{0,2},{2,0},{4,6},{6,4},{8,10},{10,8},{12,14},{14,12},{16,18},{18,... | collective-permute-start | bytes 196616 | tf_op jit(solution)/shard_map/ppermute | solution.py:209
  22.5 1.4 %collective-permute-start.9 = (f32[3,3,32,128]{3,2,1,0:T(8,128)S(1)}, f32[3,3,32,128]{3,2,1,0:T(8,128)S(1)}, u32[]{:S(2)}, u32[]{:S(2)}) collective-permute-start(f32[3,3,32,128]{3,2,1,0:T(8,128)S(1)} %forward.1.parts), channel_id=1, source_target_pairs={{0,1},{1,0},{2,3},{3,2},{4,5},{5,4},{6,7},{7,6},{8,9},{9,8},{10,11... | collective-permute-start | bytes 442376 | tf_op jit(solution)/shard_map/ppermute | solution.py:209
  26.2 5.6 %collective-permute-start.10 = (bf16[2,4,4096]{2,1,0:T(4,128)(2,1)S(1)}, bf16[2,4,4096]{2,1,0:T(4,128)(2,1)S(1)}, u32[]{:S(2)}, u32[]{:S(2)}) collective-permute-start(bf16[2,4,4096]{2,1,0:T(4,128)(2,1)S(1)} %get-tuple-element.26), channel_id=1, source_target_pairs={{0,2},{2,0},{4,6},{6,4},{8,10},{10,8},{12,14},{14,12},{16,18},{18,... | collective-permute-start | bytes 196616 | tf_op jit(solution)/shard_map/ppermute | solution.py:209
  27.0 6.2 %collective-permute-start.11 = (bf16[2,4,4096]{2,1,0:T(4,128)(2,1)S(1)}, bf16[2,4,4096]{2,1,0:T(4,128)(2,1)S(1)}, u32[]{:S(2)}, u32[]{:S(2)}) collective-permute-start(bf16[2,4,4096]{2,1,0:T(4,128)(2,1)S(1)} %get-tuple-element.27), channel_id=1, source_target_pairs={{0,4},{2,6},{4,0},{6,2},{8,12},{10,14},{12,8},{14,10},{16,20},{18,... | collective-permute-start | bytes 196616 | tf_op jit(solution)/shard_map/ppermute | solution.py:209
  28.3 5.7 %collective-permute-start.12 = (bf16[2,4,4096]{2,1,0:T(4,128)(2,1)S(1)}, bf16[2,4,4096]{2,1,0:T(4,128)(2,1)S(1)}, u32[]{:S(2)}, u32[]{:S(2)}) collective-permute-start(bf16[2,4,4096]{2,1,0:T(4,128)(2,1)S(1)} %get-tuple-element.28), channel_id=1, source_target_pairs={{0,6},{2,4},{4,2},{6,0},{8,14},{10,12},{12,10},{14,8},{16,22},{18,... | collective-permute-start | bytes 196616 | tf_op jit(solution)/shard_map/ppermute | solution.py:209
  29.7 6.2 %collective-permute-start.14 = (bf16[2,4,4096]{2,1,0:T(4,128)(2,1)S(1)}, bf16[2,4,4096]{2,1,0:T(4,128)(2,1)S(1)}, u32[]{:S(2)}, u32[]{:S(2)}) collective-permute-start(bf16[2,4,4096]{2,1,0:T(4,128)(2,1)S(1)} %get-tuple-element.30), channel_id=1, source_target_pairs={{0,2},{2,0},{4,6},{6,4},{8,10},{10,8},{12,14},{14,12},{16,18},{18,... | collective-permute-start | bytes 196616 | tf_op jit(solution)/shard_map/ppermute | solution.py:209
  30.5 5.5 %collective-permute-start.15 = (bf16[2,4,4096]{2,1,0:T(4,128)(2,1)S(1)}, bf16[2,4,4096]{2,1,0:T(4,128)(2,1)S(1)}, u32[]{:S(2)}, u32[]{:S(2)}) collective-permute-start(bf16[2,4,4096]{2,1,0:T(4,128)(2,1)S(1)} %get-tuple-element.31), channel_id=1, source_target_pairs={{0,4},{2,6},{4,0},{6,2},{8,12},{10,14},{12,8},{14,10},{16,20},{18,... | collective-permute-start | bytes 196616 | tf_op jit(solution)/shard_map/ppermute | solution.py:209
  31.8 5.2 %collective-permute-start.16 = (bf16[2,4,4096]{2,1,0:T(4,128)(2,1)S(1)}, bf16[2,4,4096]{2,1,0:T(4,128)(2,1)S(1)}, u32[]{:S(2)}, u32[]{:S(2)}) collective-permute-start(bf16[2,4,4096]{2,1,0:T(4,128)(2,1)S(1)} %get-tuple-element.32), channel_id=1, source_target_pairs={{0,6},{2,4},{4,2},{6,0},{8,14},{10,12},{12,10},{14,8},{16,22},{18,... | collective-permute-start | bytes 196616 | tf_op jit(solution)/shard_map/ppermute | solution.py:209
  34.1 10.4 %collective-permute-start.13 = (bf16[2,2,4096]{2,1,0:T(2,128)(2,1)S(1)}, bf16[2,2,4096]{2,1,0:T(2,128)(2,1)S(1)}, u32[]{:S(2)}, u32[]{:S(2)}) collective-permute-start(bf16[2,2,4096]{2,1,0:T(2,128)(2,1)S(1)} %slice.43), channel_id=1, source_target_pairs={{0,8},{2,10},{4,12},{6,14},{8,0},{10,2},{12,4},{14,6},{16,24},{18,... | collective-permute-start | bytes 98312 | tf_op jit(solution)/shard_map/ppermute | solution.py:209
  37.1 7.4 %collective-permute-start.17 = (bf16[2,2,4096]{2,1,0:T(2,128)(2,1)S(1)}, bf16[2,2,4096]{2,1,0:T(2,128)(2,1)S(1)}, u32[]{:S(2)}, u32[]{:S(2)}) collective-permute-start(bf16[2,2,4096]{2,1,0:T(2,128)(2,1)S(1)} %get-tuple-element.37), channel_id=1, source_target_pairs={{0,16},{2,18},{4,20},{6,22},{8,24},{10,26},{12,28},{14,30},{16,0},... | collective-permute-start | bytes 98312 | tf_op jit(solution)/shard_map/ppermute | solution.py:209
  40.0 5.7 %collective-permute-start.18 = (bf16[2,2,4096]{2,1,0:T(2,128)(2,1)S(1)}, bf16[2,2,4096]{2,1,0:T(2,128)(2,1)S(1)}, u32[]{:S(2)}, u32[]{:S(2)}) collective-permute-start(bf16[2,2,4096]{2,1,0:T(2,128)(2,1)S(1)} %get-tuple-element.38), channel_id=1, source_target_pairs={{0,24},{2,26},{4,28},{6,30},{8,16},{10,18},{12,20},{14,22},{16,8},... | collective-permute-start | bytes 98312 | tf_op jit(solution)/shard_map/ppermute | solution.py:209

commit v3 on v2

--- a/solution.py
+++ b/solution.py
@@ -233,7 +233,9 @@
     for part in (pieces[:half], pieces[half:]):
         halves.append(lax.optimization_barrier(jnp.concatenate(part, axis=1)))
     quarter_rows = [[part] + [swap(part, offset) for offset in stages[0][1:]] for part in halves]
-    panels = [lax.optimization_barrier(jnp.concatenate(part, axis=1)) for part in quarter_rows]
+    panels = []
+    for part in quarter_rows:
+        panels.append(lax.optimization_barrier(jnp.concatenate(part, axis=1)))
 
     parts = pl.pallas_call(
         functools.partial(forward_kernel, group),
@@ -291,19 +293,18 @@
             blocks[h * count + i] = total[:, i * step:(i + 1) * step]
             if h * count + i:
                 blocks[h * count + i] = blocks[h * count + i].astype(BF16)
-    total = blocks[0]
-    for i, offset in enumerate(stages[1][1:], 1):
-        total = total + swap(blocks[i], offset).astype(F32)
-    for stage in stages[2:]:
-        size = total.shape[1] // len(stage)
-        pieces = [total[:, q * size:(q + 1) * size] for q in range(len(stage))]
-        total = pieces[0]
-        for piece, offset in zip(pieces[1:], stage[1:]):
-            total = total + swap(piece.astype(BF16), offset).astype(F32)
-    total = total.astype(BF16)
+    pieces = [blocks[i] for i in range(len(stages[1]))]
+    for stage, following in zip(stages[1:], stages[2:] + [None]):
+        came = [swap(piece.astype(BF16), offset) for piece, offset in zip(pieces[1:], stage[1:])]
+        sums = [sum((c[w].astype(F32) for c in came), pieces[0][w]) for w in range(2)]
+        if following:
+            total = jnp.stack(sums)
+            size = total.shape[1] // len(following)
+            pieces = [total[:, q * size:(q + 1) * size] for q in range(len(following))]
+    layer_out, input_grad = [value.astype(BF16) for value in sums]
     gate_grad, up_grad, down_grad = tile_grads(((0, 0), (1, 0), (2, 1)))
     grads = [g[None, None] for g in (gate_grad, up_grad, down_grad)]
-    return (total[0], total[1], *grads)
+    return (layer_out, input_grad, *grads)
 
 
 def solution(mesh):

time: 46.7 us -> 46.7 us (level)
  local copies, waits for them, and re-layouts: 0.72 us -> 0.09 us
  other arithmetic: 1.4 us -> 2.01 us
    add x0 -> x1, other arithmetic: none -> 0.68 us  [per_device(): sum((c[w].astype(F32) for c in came), pieces[0][w])]
    squeeze x1 -> x0, local copies, waits for them, and re-layouts: 0.64 us -> none  [per_device(): return (total[0], total[1], *grads)]
where the time goes in v3:
time: 46.7 us; the launch traced here: 46.3 us
  starting transfers between devices  26.3 us (56%)
  Pallas kernels  9.6 us (21%)
  waiting for transfers between devices  7.62 us (16%)
  other arithmetic  2.01 us (4%)
  between operations  0.75 us (2%)
    ppermute x19, starting transfers between devices, swap(): return lax.ppermute(x, axis, [(i, i ^ bit) for i in range(size)])  26.3 us
    ppermute x19, waiting for transfers between devices, swap(): return lax.ppermute(x, axis, [(i, i ^ bit) for i in range(size)])  7.62 us
    pallas_call x1, Pallas kernels, tile_grads(): pl.pallas_call(functools.partial(grad_kernel, group, jobs), out_shape=[ja...  3.17 us
    pallas_call x1, Pallas kernels, per_device(): pl.pallas_call(functools.partial(load_kernel, row_blocks), out_shape=[plt...  2.41 us
    pallas_call x1, Pallas kernels, per_device(): pl.pallas_call(functools.partial(backward_kernel, group, quarters), out_s...  2.21 us
    pallas_call x1, Pallas kernels, per_device(): pl.pallas_call(functools.partial(forward_kernel, group), out_shape=pltpu....  1.8 us
  transfers between devices with their start and end apart: 19, of which 8 were waited for; matrix products, arithmetic and copies ran while one was open for 1% of the time, Pallas kernels for 12%

profile of v3, /device:TPU:0, one launch (start us, length us, event | category | flops | bytes accessed | tf_op | source)
XLA Modules:
  0.0 46.3 jit_solution(16830856570265991614)
XLA Ops:
  0.6 0.8 %pad_maximum_fusion.4 = bf16[2,2,4096]{2,1,0:T(2,128)(2,1)S(1)} fusion(bf16[1,2,4096]{2,1,0:T(2,128)(2,1)} %bitcast.28, bf16[1,2,4096]{2,1,0:T(2,128)(2,1)} %bitcast.29), kind=kLoop, calls=%fused_computation.13 | loop fusion | flops 16384 | bytes 65536 | tf_op jit(solution)/shard_map/stack | solution.py:226
  1.4 3.1 %collective-permute-start = (bf16[2,2,4096]{2,1,0:T(2,128)(2,1)S(1)}, bf16[2,2,4096]{2,1,0:T(2,128)(2,1)S(1)}, u32[]{:S(2)}, u32[]{:S(2)}) collective-permute-start(bf16[2,2,4096]{2,1,0:T(2,128)(2,1)S(1)} %pad_maximum_fusion.4), channel_id=1, source_target_pairs={{0,8},{2,10},{4,12},{6,14},{8,0},{10,2},{12,4},{14,6},{16,24},{18,... | collective-permute-start | bytes 98312 | tf_op jit(solution)/shard_map/ppermute | solution.py:209
  4.5 2.5 %collective-permute-start.5 = (bf16[2,2,4096]{2,1,0:T(2,128)(2,1)S(1)}, bf16[2,2,4096]{2,1,0:T(2,128)(2,1)S(1)}, u32[]{:S(2)}, u32[]{:S(2)}) collective-permute-start(bf16[2,2,4096]{2,1,0:T(2,128)(2,1)S(1)} %pad_maximum_fusion.4), channel_id=1, source_target_pairs={{0,24},{2,26},{4,28},{6,30},{8,16},{10,18},{12,20},{14,22},{16,8},... | collective-permute-start | bytes 98312 | tf_op jit(solution)/shard_map/ppermute | solution.py:209
  7.0 0.1 collective-permute-start.4
  7.1 2.4 %load.1 = (bf16[48,128,128]{2,1,0:T(8,128)(2,1)S(1)}, bf16[48,128,128]{2,1,0:T(8,128)(2,1)S(1)}, bf16[48,128,128]{2,1,0:T(8,128)(2,1)S(1)}, s32[3,2,48]{2,1,0:T(2,128)S(1)}) custom-call(s32[3,1,48]{2,1,0:T(1,128)} %bitcast.30, s32[3]{0:T(128)} %bitcast.31, bf16[48,128,128]{2,1,0:T(8,128)(2,1)} %bitcast.20, bf16[48,128,128]{2,1,0:T(8,128)(2,1)} %bitcast.21, ...), custom_call_target="tpu_custom_call" | custom-call | tf_op jit(solution)/shard_map/load/pallas_call | solution.py:211
  9.5 0.0 collective-permute-done
  9.6 0.1 pad_maximum_fusion.2
  9.6 2.5 %collective-permute-start.3 = (bf16[2,4,4096]{2,1,0:T(4,128)(2,1)S(1)}, bf16[2,4,4096]{2,1,0:T(4,128)(2,1)S(1)}, u32[]{:S(2)}, u32[]{:S(2)}) collective-permute-start(bf16[2,4,4096]{2,1,0:T(4,128)(2,1)S(1)} %pad_maximum_fusion.2), channel_id=1, source_target_pairs={{0,6},{2,4},{4,2},{6,0},{8,14},{10,12},{12,10},{14,8},{16,22},{18,... | collective-permute-start | bytes 196616 | tf_op jit(solution)/shard_map/ppermute | solution.py:209
  12.2 0.5 %collective-permute-start.2 = (bf16[2,4,4096]{2,1,0:T(4,128)(2,1)S(1)}, bf16[2,4,4096]{2,1,0:T(4,128)(2,1)S(1)}, u32[]{:S(2)}, u32[]{:S(2)}) collective-permute-start(bf16[2,4,4096]{2,1,0:T(4,128)(2,1)S(1)} %pad_maximum_fusion.2), channel_id=1, source_target_pairs={{0,4},{2,6},{4,0},{6,2},{8,12},{10,14},{12,8},{14,10},{16,20},{18,... | collective-permute-start | bytes 196616 | tf_op jit(solution)/shard_map/ppermute | solution.py:209
  12.7 0.5 %collective-permute-start.1 = (bf16[2,4,4096]{2,1,0:T(4,128)(2,1)S(1)}, bf16[2,4,4096]{2,1,0:T(4,128)(2,1)S(1)}, u32[]{:S(2)}, u32[]{:S(2)}) collective-permute-start(bf16[2,4,4096]{2,1,0:T(4,128)(2,1)S(1)} %pad_maximum_fusion.2), channel_id=1, source_target_pairs={{0,2},{2,0},{4,6},{6,4},{8,10},{10,8},{12,14},{14,12},{16,18},{18,... | collective-permute-start | bytes 196616 | tf_op jit(solution)/shard_map/ppermute | solution.py:209
  13.2 0.0 collective-permute-done.5
  13.2 0.0 collective-permute-done.4
  13.2 0.1 pad_maximum_fusion.3
  13.3 2.5 %collective-permute-start.8 = (bf16[2,4,4096]{2,1,0:T(4,128)(2,1)S(1)}, bf16[2,4,4096]{2,1,0:T(4,128)(2,1)S(1)}, u32[]{:S(2)}, u32[]{:S(2)}) collective-permute-start(bf16[2,4,4096]{2,1,0:T(4,128)(2,1)S(1)} %pad_maximum_fusion.3), channel_id=1, source_target_pairs={{0,6},{2,4},{4,2},{6,0},{8,14},{10,12},{12,10},{14,8},{16,22},{18,... | collective-permute-start | bytes 196616 | tf_op jit(solution)/shard_map/ppermute | solution.py:209
  15.8 0.5 %collective-permute-start.7 = (bf16[2,4,4096]{2,1,0:T(4,128)(2,1)S(1)}, bf16[2,4,4096]{2,1,0:T(4,128)(2,1)S(1)}, u32[]{:S(2)}, u32[]{:S(2)}) collective-permute-start(bf16[2,4,4096]{2,1,0:T(4,128)(2,1)S(1)} %pad_maximum_fusion.3), channel_id=1, source_target_pairs={{0,4},{2,6},{4,0},{6,2},{8,12},{10,14},{12,8},{14,10},{16,20},{18,... | collective-permute-start | bytes 196616 | tf_op jit(solution)/shard_map/ppermute | solution.py:209
  16.3 0.0 collective-permute-done.3
  16.3 0.8 %collective-permute-start.6 = (bf16[2,4,4096]{2,1,0:T(4,128)(2,1)S(1)}, bf16[2,4,4096]{2,1,0:T(4,128)(2,1)S(1)}, u32[]{:S(2)}, u32[]{:S(2)}) collective-permute-start(bf16[2,4,4096]{2,1,0:T(4,128)(2,1)S(1)} %pad_maximum_fusion.3), channel_id=1, source_target_pairs={{0,2},{2,0},{4,6},{6,4},{8,10},{10,8},{12,14},{14,12},{16,18},{18,... | collective-permute-start | bytes 196616 | tf_op jit(solution)/shard_map/ppermute | solution.py:209
  17.1 0.5 collective-permute-done.2
  17.5 0.0 collective-permute-done.1
  17.5 0.2 pad_maximum_fusion.panel_a
  17.7 1.6 %collective-permute-done.8 = bf16[2,4,4096]{2,1,0:T(4,128)(2,1)S(1)} collective-permute-done((bf16[2,4,4096]{2,1,0:T(4,128)(2,1)S(1)}, bf16[2,4,4096]{2,1,0:T(4,128)(2,1)S(1)}, u32[]{:S(2)}, u32[]{:S(2)}) %collective-permute-start.8) | collective-permute-done | bytes 65568 | tf_op jit(solution)/shard_map/ppermute | solution.py:209
  19.3 0.8 %collective-permute-done.7 = bf16[2,4,4096]{2,1,0:T(4,128)(2,1)S(1)} collective-permute-done((bf16[2,4,4096]{2,1,0:T(4,128)(2,1)S(1)}, bf16[2,4,4096]{2,1,0:T(4,128)(2,1)S(1)}, u32[]{:S(2)}, u32[]{:S(2)}) %collective-permute-start.7) | collective-permute-done | bytes 65568 | tf_op jit(solution)/shard_map/ppermute | solution.py:209
  20.1 0.5 %collective-permute-done.6 = bf16[2,4,4096]{2,1,0:T(4,128)(2,1)S(1)} collective-permute-done((bf16[2,4,4096]{2,1,0:T(4,128)(2,1)S(1)}, bf16[2,4,4096]{2,1,0:T(4,128)(2,1)S(1)}, u32[]{:S(2)}, u32[]{:S(2)}) %collective-permute-start.6) | collective-permute-done | bytes 65568 | tf_op jit(solution)/shard_map/ppermute | solution.py:209
  20.6 0.2 pad_maximum_fusion.1.panel_b
  20.7 1.8 %forward.1.parts = f32[3,3,32,128]{3,2,1,0:T(8,128)S(1)} custom-call(s32[3,2,48]{2,1,0:T(2,128)S(1)} %get-tuple-element.21.idx, bf16[2,16,4096]{2,1,0:T(8,128)(2,1)S(1)} %pad_maximum_fusion.panel_a, bf16[2,16,4096]{2,1,0:T(8,128)(2,1)S(1)} %pad_maximum_fusion.1.panel_b, bf16[48,128,128]{2,1,0:T(8,128)(2,1)S(1)} %get-tuple-element.22.gate, ...), custom_call_target="tpu_custom_call" | custom-call | tf_op jit(solution)/shard_map/forward/pallas_call | solution.py:240
  22.5 0.1 collective-permute-start.9
  22.6 1.4 %collective-permute-done.9.other = f32[3,3,32,128]{3,2,1,0:T(8,128)S(1)} collective-permute-done((f32[3,3,32,128]{3,2,1,0:T(8,128)S(1)}, f32[3,3,32,128]{3,2,1,0:T(8,128)S(1)}, u32[]{:S(2)}, u32[]{:S(2)}) %collective-permute-start.9) | collective-permute-done | bytes 147488 | tf_op jit(solution)/shard_map/ppermute | solution.py:209
  24.0 2.2 %backward.1 = (bf16[3,4,32,128]{3,2,1,0:T(8,128)(2,1)S(1)}, f32[2,4,4096]{2,1,0:T(4,128)S(1)}, f32[2,4,4096]{2,1,0:T(4,128)S(1)}, bf16[2,4,4096]{2,1,0:T(4,128)(...) custom-call(s32[3,2,48]{2,1,0:T(2,128)S(1)} %get-tuple-element.21.id, ...), custom_call_target="tpu_custom_call" | custom-call | tf_op jit(solution)/shard_map/backward/pallas_call | solution.py:255
  26.2 0.8 %collective-permute-start.10 = (bf16[2,4,4096]{2,1,0:T(4,128)(2,1)S(1)}, bf16[2,4,4096]{2,1,0:T(4,128)(2,1)S(1)}, u32[]{:S(2)}, u32[]{:S(2)}) collective-permute-start(bf16[2,4,4096]{2,1,0:T(4,128)(2,1)S(1)} %get-tuple-element.26), channel_id=1, source_target_pairs={{0,2},{2,0},{4,6},{6,4},{8,10},{10,8},{12,14},{14,12},{16,18},{18,... | collective-permute-start | bytes 196616 | tf_op jit(solution)/shard_map/ppermute | solution.py:209
  27.0 1.3 %collective-permute-start.11 = (bf16[2,4,4096]{2,1,0:T(4,128)(2,1)S(1)}, bf16[2,4,4096]{2,1,0:T(4,128)(2,1)S(1)}, u32[]{:S(2)}, u32[]{:S(2)}) collective-permute-start(bf16[2,4,4096]{2,1,0:T(4,128)(2,1)S(1)} %get-tuple-element.27), channel_id=1, source_target_pairs={{0,4},{2,6},{4,0},{6,2},{8,12},{10,14},{12,8},{14,10},{16,20},{18,... | collective-permute-start | bytes 196616 | tf_op jit(solution)/shard_map/ppermute | solution.py:209
  28.3 1.4 %collective-permute-start.12 = (bf16[2,4,4096]{2,1,0:T(4,128)(2,1)S(1)}, bf16[2,4,4096]{2,1,0:T(4,128)(2,1)S(1)}, u32[]{:S(2)}, u32[]{:S(2)}) collective-permute-start(bf16[2,4,4096]{2,1,0:T(4,128)(2,1)S(1)} %get-tuple-element.28), channel_id=1, source_target_pairs={{0,6},{2,4},{4,2},{6,0},{8,14},{10,12},{12,10},{14,8},{16,22},{18,... | collective-permute-start | bytes 196616 | tf_op jit(solution)/shard_map/ppermute | solution.py:209
  29.7 0.7 %collective-permute-start.14 = (bf16[2,4,4096]{2,1,0:T(4,128)(2,1)S(1)}, bf16[2,4,4096]{2,1,0:T(4,128)(2,1)S(1)}, u32[]{:S(2)}, u32[]{:S(2)}) collective-permute-start(bf16[2,4,4096]{2,1,0:T(4,128)(2,1)S(1)} %get-tuple-element.30), channel_id=1, source_target_pairs={{0,2},{2,0},{4,6},{6,4},{8,10},{10,8},{12,14},{14,12},{16,18},{18,... | collective-permute-start | bytes 196616 | tf_op jit(solution)/shard_map/ppermute | solution.py:209
  30.5 1.3 %collective-permute-start.15 = (bf16[2,4,4096]{2,1,0:T(4,128)(2,1)S(1)}, bf16[2,4,4096]{2,1,0:T(4,128)(2,1)S(1)}, u32[]{:S(2)}, u32[]{:S(2)}) collective-permute-start(bf16[2,4,4096]{2,1,0:T(4,128)(2,1)S(1)} %get-tuple-element.31), channel_id=1, source_target_pairs={{0,4},{2,6},{4,0},{6,2},{8,12},{10,14},{12,8},{14,10},{16,20},{18,... | collective-permute-start | bytes 196616 | tf_op jit(solution)/shard_map/ppermute | solution.py:209
  31.8 1.4 %collective-permute-start.16 = (bf16[2,4,4096]{2,1,0:T(4,128)(2,1)S(1)}, bf16[2,4,4096]{2,1,0:T(4,128)(2,1)S(1)}, u32[]{:S(2)}, u32[]{:S(2)}) collective-permute-start(bf16[2,4,4096]{2,1,0:T(4,128)(2,1)S(1)} %get-tuple-element.32), channel_id=1, source_target_pairs={{0,6},{2,4},{4,2},{6,0},{8,14},{10,12},{12,10},{14,8},{16,22},{18,... | collective-permute-start | bytes 196616 | tf_op jit(solution)/shard_map/ppermute | solution.py:209
  33.2 0.0 collective-permute-done.11
  33.2 0.8 %collective-permute-done.12 = bf16[2,4,4096]{2,1,0:T(4,128)(2,1)S(1)} collective-permute-done((bf16[2,4,4096]{2,1,0:T(4,128)(2,1)S(1)}, bf16[2,4,4096]{2,1,0:T(4,128)(2,1)S(1)}, u32[]{:S(2)}, u32[]{:S(2)}) %collective-permute-start.12) | collective-permute-done | bytes 65568 | tf_op jit(solution)/shard_map/ppermute | solution.py:209
  34.1 1.9 %collective-permute-start.13 = (bf16[2,2,4096]{2,1,0:T(2,128)(2,1)S(1)}, bf16[2,2,4096]{2,1,0:T(2,128)(2,1)S(1)}, u32[]{:S(2)}, u32[]{:S(2)}) collective-permute-start(bf16[2,2,4096]{2,1,0:T(2,128)(2,1)S(1)} %slice.98), channel_id=1, source_target_pairs={{0,8},{2,10},{4,12},{6,14},{8,0},{10,2},{12,4},{14,6},{16,24},{18,... | collective-permute-start | bytes 98312 | tf_op jit(solution)/shard_map/ppermute | solution.py:209
  36.0 0.0 collective-permute-done.14
  36.0 0.0 collective-permute-done.15
  36.0 1.0 %collective-permute-done.16 = bf16[2,4,4096]{2,1,0:T(4,128)(2,1)S(1)} collective-permute-done((bf16[2,4,4096]{2,1,0:T(4,128)(2,1)S(1)}, bf16[2,4,4096]{2,1,0:T(4,128)(2,1)S(1)}, u32[]{:S(2)}, u32[]{:S(2)}) %collective-permute-start.16) | collective-permute-done | bytes 65568 | tf_op jit(solution)/shard_map/ppermute | solution.py:209
  37.0 0.1 add_convert_fusion
  37.1 2.9 %collective-permute-start.17 = (bf16[2,2,4096]{2,1,0:T(2,128)(2,1)S(1)}, bf16[2,2,4096]{2,1,0:T(2,128)(2,1)S(1)}, u32[]{:S(2)}, u32[]{:S(2)}) collective-permute-start(bf16[2,2,4096]{2,1,0:T(2,128)(2,1)S(1)} %get-tuple-element.39), channel_id=1, source_target_pairs={{0,16},{2,18},{4,20},{6,22},{8,24},{10,26},{12,28},{14,30},{16,0},... | collective-permute-start | bytes 98312 | tf_op jit(solution)/shard_map/ppermute | solution.py:209
  40.0 1.4 %collective-permute-start.18 = (bf16[2,2,4096]{2,1,0:T(2,128)(2,1)S(1)}, bf16[2,2,4096]{2,1,0:T(2,128)(2,1)S(1)}, u32[]{:S(2)}, u32[]{:S(2)}) collective-permute-start(bf16[2,2,4096]{2,1,0:T(2,128)(2,1)S(1)} %get-tuple-element.40), channel_id=1, source_target_pairs={{0,24},{2,26},{4,28},{6,30},{8,16},{10,18},{12,20},{14,22},{16,8},... | collective-permute-start | bytes 98312 | tf_op jit(solution)/shard_map/ppermute | solution.py:209
  41.3 3.2 %shard_map.110 = (bf16[48,128,128]{2,1,0:T(8,128)(2,1)}, bf16[48,128,128]{2,1,0:T(8,128)(2,1)}, bf16[48,128,128]{2,1,0:T(8,128)(2,1)}) custom-call(s32[3,2,48]{2,1,0:T(2,128)S(1)} %get-tuple-element.21.idx, bf16[2,16,4096]{2,1,0:T(8,128)(2,1)S(1)} %pad_maximum_fusion.panel_a, bf16[2,16,4096]{2,1,0:T(8,128)(2,1)S(1)} %pad_maximum_fusion.1.panel_b, ...), custom_call_target="tpu_custom_call" | custom-call | flops 150994944 | bytes 9437184 | tf_op jit(solution)/shard_map/pallas_call | solution.py:269
  44.5 0.0 collective-permute-done.13
  44.5 0.0 collective-permute-done.17
  44.5 1.2 %collective-permute-done.18 = bf16[2,2,4096]{2,1,0:T(2,128)(2,1)S(1)} collective-permute-done((bf16[2,2,4096]{2,1,0:T(2,128)(2,1)S(1)}, bf16[2,2,4096]{2,1,0:T(2,128)(2,1)S(1)}, u32[]{:S(2)}, u32[]{:S(2)}) %collective-permute-start.18) | collective-permute-done | bytes 32800 | tf_op jit(solution)/shard_map/ppermute | solution.py:209
  45.7 0.7 %fusion.6 = (bf16[2,4096]{1,0:T(2,128)(2,1)}, bf16[2,4096]{1,0:T(2,128)(2,1)}) fusion(bf16[2,2,4096]{2,1,0:T(2,128)(2,1)S(1)} %collective-permute-done.18, bf16[2,2,4096]{2,1,0:T(2,128)(2,1)S(1)} %collective-permute-done.17, bf16[2,2,4096]{2,1,0:T(2,128)(2,1)S(1)} %collective-permute-done.13, f32[2,4,4096]{2,1,0:T(4,128)S(1)} %bitcast.24), kind=kLoop, calls=%fused_computation.16 | loop fusion | flops 114688 | bytes 196608 | tf_op jit(solution)/shard_map/add | solution.py:299
  (4 shorter events, 0.1 us)
Async XLA Ops:
  1.4 8.1 %collective-permute-start = (bf16[2,2,4096]{2,1,0:T(2,128)(2,1)S(1)}, bf16[2,2,4096]{2,1,0:T(2,128)(2,1)S(1)}, u32[]{:S(2)}, u32[]{:S(2)}) collective-permute-start(bf16[2,2,4096]{2,1,0:T(2,128)(2,1)S(1)} %pad_maximum_fusion.4), channel_id=1, source_target_pairs={{0,8},{2,10},{4,12},{6,14},{8,0},{10,2},{12,4},{14,6},{16,24},{18,... | collective-permute-start | bytes 98312 | tf_op jit(solution)/shard_map/ppermute | solution.py:209
  4.5 8.7 %collective-permute-start.5 = (bf16[2,2,4096]{2,1,0:T(2,128)(2,1)S(1)}, bf16[2,2,4096]{2,1,0:T(2,128)(2,1)S(1)}, u32[]{:S(2)}, u32[]{:S(2)}) collective-permute-start(bf16[2,2,4096]{2,1,0:T(2,128)(2,1)S(1)} %pad_maximum_fusion.4), channel_id=1, source_target_pairs={{0,24},{2,26},{4,28},{6,30},{8,16},{10,18},{12,20},{14,22},{16,8},... | collective-permute-start | bytes 98312 | tf_op jit(solution)/shard_map/ppermute | solution.py:209
  7.0 6.2 %collective-permute-start.4 = (bf16[2,2,4096]{2,1,0:T(2,128)(2,1)S(1)}, bf16[2,2,4096]{2,1,0:T(2,128)(2,1)S(1)}, u32[]{:S(2)}, u32[]{:S(2)}) collective-permute-start(bf16[2,2,4096]{2,1,0:T(2,128)(2,1)S(1)} %pad_maximum_fusion.4), channel_id=1, source_target_pairs={{0,16},{2,18},{4,20},{6,22},{8,24},{10,26},{12,28},{14,30},{16,0},... | collective-permute-start | bytes 98312 | tf_op jit(solution)/shard_map/ppermute | solution.py:209
  9.6 6.7 %collective-permute-start.3 = (bf16[2,4,4096]{2,1,0:T(4,128)(2,1)S(1)}, bf16[2,4,4096]{2,1,0:T(4,128)(2,1)S(1)}, u32[]{:S(2)}, u32[]{:S(2)}) collective-permute-start(bf16[2,4,4096]{2,1,0:T(4,128)(2,1)S(1)} %pad_maximum_fusion.2), channel_id=1, source_target_pairs={{0,6},{2,4},{4,2},{6,0},{8,14},{10,12},{12,10},{14,8},{16,22},{18,... | collective-permute-start | bytes 196616 | tf_op jit(solution)/shard_map/ppermute | solution.py:209
  12.2 5.4 %collective-permute-start.2 = (bf16[2,4,4096]{2,1,0:T(4,128)(2,1)S(1)}, bf16[2,4,4096]{2,1,0:T(4,128)(2,1)S(1)}, u32[]{:S(2)}, u32[]{:S(2)}) collective-permute-start(bf16[2,4,4096]{2,1,0:T(4,128)(2,1)S(1)} %pad_maximum_fusion.2), channel_id=1, source_target_pairs={{0,4},{2,6},{4,0},{6,2},{8,12},{10,14},{12,8},{14,10},{16,20},{18,... | collective-permute-start | bytes 196616 | tf_op jit(solution)/shard_map/ppermute | solution.py:209
  12.7 4.9 %collective-permute-start.1 = (bf16[2,4,4096]{2,1,0:T(4,128)(2,1)S(1)}, bf16[2,4,4096]{2,1,0:T(4,128)(2,1)S(1)}, u32[]{:S(2)}, u32[]{:S(2)}) collective-permute-start(bf16[2,4,4096]{2,1,0:T(4,128)(2,1)S(1)} %pad_maximum_fusion.2), channel_id=1, source_target_pairs={{0,2},{2,0},{4,6},{6,4},{8,10},{10,8},{12,14},{14,12},{16,18},{18,... | collective-permute-start | bytes 196616 | tf_op jit(solution)/shard_map/ppermute | solution.py:209
  13.3 6.0 %collective-permute-start.8 = (bf16[2,4,4096]{2,1,0:T(4,128)(2,1)S(1)}, bf16[2,4,4096]{2,1,0:T(4,128)(2,1)S(1)}, u32[]{:S(2)}, u32[]{:S(2)}) collective-permute-start(bf16[2,4,4096]{2,1,0:T(4,128)(2,1)S(1)} %pad_maximum_fusion.3), channel_id=1, source_target_pairs={{0,6},{2,4},{4,2},{6,0},{8,14},{10,12},{12,10},{14,8},{16,22},{18,... | collective-permute-start | bytes 196616 | tf_op jit(solution)/shard_map/ppermute | solution.py:209
  15.8 4.3 %collective-permute-start.7 = (bf16[2,4,4096]{2,1,0:T(4,128)(2,1)S(1)}, bf16[2,4,4096]{2,1,0:T(4,128)(2,1)S(1)}, u32[]{:S(2)}, u32[]{:S(2)}) collective-permute-start(bf16[2,4,4096]{2,1,0:T(4,128)(2,1)S(1)} %pad_maximum_fusion.3), channel_id=1, source_target_pairs={{0,4},{2,6},{4,0},{6,2},{8,12},{10,14},{12,8},{14,10},{16,20},{18,... | collective-permute-start | bytes 196616 | tf_op jit(solution)/shard_map/ppermute | solution.py:209
  16.3 4.3 %collective-permute-start.6 = (bf16[2,4,4096]{2,1,0:T(4,128)(2,1)S(1)}, bf16[2,4,4096]{2,1,0:T(4,128)(2,1)S(1)}, u32[]{:S(2)}, u32[]{:S(2)}) collective-permute-start(bf16[2,4,4096]{2,1,0:T(4,128)(2,1)S(1)} %pad_maximum_fusion.3), channel_id=1, source_target_pairs={{0,2},{2,0},{4,6},{6,4},{8,10},{10,8},{12,14},{14,12},{16,18},{18,... | collective-permute-start | bytes 196616 | tf_op jit(solution)/shard_map/ppermute | solution.py:209
  22.5 1.4 %collective-permute-start.9 = (f32[3,3,32,128]{3,2,1,0:T(8,128)S(1)}, f32[3,3,32,128]{3,2,1,0:T(8,128)S(1)}, u32[]{:S(2)}, u32[]{:S(2)}) collective-permute-start(f32[3,3,32,128]{3,2,1,0:T(8,128)S(1)} %forward.1.parts), channel_id=1, source_target_pairs={{0,1},{1,0},{2,3},{3,2},{4,5},{5,4},{6,7},{7,6},{8,9},{9,8},{10,11... | collective-permute-start | bytes 442376 | tf_op jit(solution)/shard_map/ppermute | solution.py:209
  26.2 5.6 %collective-permute-start.10 = (bf16[2,4,4096]{2,1,0:T(4,128)(2,1)S(1)}, bf16[2,4,4096]{2,1,0:T(4,128)(2,1)S(1)}, u32[]{:S(2)}, u32[]{:S(2)}) collective-permute-start(bf16[2,4,4096]{2,1,0:T(4,128)(2,1)S(1)} %get-tuple-element.26), channel_id=1, source_target_pairs={{0,2},{2,0},{4,6},{6,4},{8,10},{10,8},{12,14},{14,12},{16,18},{18,... | collective-permute-start | bytes 196616 | tf_op jit(solution)/shard_map/ppermute | solution.py:209
  27.0 6.2 %collective-permute-start.11 = (bf16[2,4,4096]{2,1,0:T(4,128)(2,1)S(1)}, bf16[2,4,4096]{2,1,0:T(4,128)(2,1)S(1)}, u32[]{:S(2)}, u32[]{:S(2)}) collective-permute-start(bf16[2,4,4096]{2,1,0:T(4,128)(2,1)S(1)} %get-tuple-element.27), channel_id=1, source_target_pairs={{0,4},{2,6},{4,0},{6,2},{8,12},{10,14},{12,8},{14,10},{16,20},{18,... | collective-permute-start | bytes 196616 | tf_op jit(solution)/shard_map/ppermute | solution.py:209
  28.3 5.7 %collective-permute-start.12 = (bf16[2,4,4096]{2,1,0:T(4,128)(2,1)S(1)}, bf16[2,4,4096]{2,1,0:T(4,128)(2,1)S(1)}, u32[]{:S(2)}, u32[]{:S(2)}) collective-permute-start(bf16[2,4,4096]{2,1,0:T(4,128)(2,1)S(1)} %get-tuple-element.28), channel_id=1, source_target_pairs={{0,6},{2,4},{4,2},{6,0},{8,14},{10,12},{12,10},{14,8},{16,22},{18,... | collective-permute-start | bytes 196616 | tf_op jit(solution)/shard_map/ppermute | solution.py:209
  29.7 6.2 %collective-permute-start.14 = (bf16[2,4,4096]{2,1,0:T(4,128)(2,1)S(1)}, bf16[2,4,4096]{2,1,0:T(4,128)(2,1)S(1)}, u32[]{:S(2)}, u32[]{:S(2)}) collective-permute-start(bf16[2,4,4096]{2,1,0:T(4,128)(2,1)S(1)} %get-tuple-element.30), channel_id=1, source_target_pairs={{0,2},{2,0},{4,6},{6,4},{8,10},{10,8},{12,14},{14,12},{16,18},{18,... | collective-permute-start | bytes 196616 | tf_op jit(solution)/shard_map/ppermute | solution.py:209
  30.5 5.5 %collective-permute-start.15 = (bf16[2,4,4096]{2,1,0:T(4,128)(2,1)S(1)}, bf16[2,4,4096]{2,1,0:T(4,128)(2,1)S(1)}, u32[]{:S(2)}, u32[]{:S(2)}) collective-permute-start(bf16[2,4,4096]{2,1,0:T(4,128)(2,1)S(1)} %get-tuple-element.31), channel_id=1, source_target_pairs={{0,4},{2,6},{4,0},{6,2},{8,12},{10,14},{12,8},{14,10},{16,20},{18,... | collective-permute-start | bytes 196616 | tf_op jit(solution)/shard_map/ppermute | solution.py:209
  31.8 5.2 %collective-permute-start.16 = (bf16[2,4,4096]{2,1,0:T(4,128)(2,1)S(1)}, bf16[2,4,4096]{2,1,0:T(4,128)(2,1)S(1)}, u32[]{:S(2)}, u32[]{:S(2)}) collective-permute-start(bf16[2,4,4096]{2,1,0:T(4,128)(2,1)S(1)} %get-tuple-element.32), channel_id=1, source_target_pairs={{0,6},{2,4},{4,2},{6,0},{8,14},{10,12},{12,10},{14,8},{16,22},{18,... | collective-permute-start | bytes 196616 | tf_op jit(solution)/shard_map/ppermute | solution.py:209
  34.1 10.4 %collective-permute-start.13 = (bf16[2,2,4096]{2,1,0:T(2,128)(2,1)S(1)}, bf16[2,2,4096]{2,1,0:T(2,128)(2,1)S(1)}, u32[]{:S(2)}, u32[]{:S(2)}) collective-permute-start(bf16[2,2,4096]{2,1,0:T(2,128)(2,1)S(1)} %slice.98), channel_id=1, source_target_pairs={{0,8},{2,10},{4,12},{6,14},{8,0},{10,2},{12,4},{14,6},{16,24},{18,... | collective-permute-start | bytes 98312 | tf_op jit(solution)/shard_map/ppermute | solution.py:209
  37.1 7.4 %collective-permute-start.17 = (bf16[2,2,4096]{2,1,0:T(2,128)(2,1)S(1)}, bf16[2,2,4096]{2,1,0:T(2,128)(2,1)S(1)}, u32[]{:S(2)}, u32[]{:S(2)}) collective-permute-start(bf16[2,2,4096]{2,1,0:T(2,128)(2,1)S(1)} %get-tuple-element.39), channel_id=1, source_target_pairs={{0,16},{2,18},{4,20},{6,22},{8,24},{10,26},{12,28},{14,30},{16,0},... | collective-permute-start | bytes 98312 | tf_op jit(solution)/shard_map/ppermute | solution.py:209
  40.0 5.7 %collective-permute-start.18 = (bf16[2,2,4096]{2,1,0:T(2,128)(2,1)S(1)}, bf16[2,2,4096]{2,1,0:T(2,128)(2,1)S(1)}, u32[]{:S(2)}, u32[]{:S(2)}) collective-permute-start(bf16[2,2,4096]{2,1,0:T(2,128)(2,1)S(1)} %get-tuple-element.40), channel_id=1, source_target_pairs={{0,24},{2,26},{4,28},{6,30},{8,16},{10,18},{12,20},{14,22},{16,8},... | collective-permute-start | bytes 98312 | tf_op jit(solution)/shard_map/ppermute | solution.py:209
